TPU v7x, 256 devices: a whole 4x4x8 slice. The times are simulated.
256 devices in a mesh: dp: 16 (over z, y_hi), tensor: 16 (over y_lo, x, core).
Axes of the slice: x: 4, y: 4 (y_hi: 2, y_lo: 2; y = y_hi * 2 + y_lo), z: 8, core: 2. Of those that a mesh axis runs over, the one named last changes fastest.
Arguments:
- picture_averaged_encodings: bfloat16 [12288, 1152], P('dp'), may hold values from -6 to 6
- caption_averaged_encodings: bfloat16 [12288, 1152], P('dp'), may hold values from -6 to 6
- picture_mapping_matrix: bfloat16 [1152, 1152], P(None, 'tensor'), may hold values from -0.1875 to 0.1875
- caption_mapping_matrix: bfloat16 [1152, 1152], P(None, 'tensor'), may hold values from -0.1875 to 0.1875
- picture_weight_perturbation: bfloat16 [1152, 1152], P(None, 'tensor'), may hold values from -0.1875 to 0.1875
- caption_weight_perturbation: bfloat16 [1152, 1152], P(None, 'tensor'), may hold values from -0.1875 to 0.1875
- sharpness_multiplier: float32 [1], replicated, may hold values from 6 to 14
- offset_additive: float32 [1], replicated, may hold values from -8 to -4
Outputs:
- image_hvp: float32 [1152, 1152], P('dp', 'tensor')
- text_hvp: float32 [1152, 1152], P('dp', 'tensor')
All inputs are finite; a program needn't handle non-finite values.
Results may differ from a plain program's by a relative error of at most 0.0025.
Values may be sent and summed in bfloat16 or wider, within the bound.
A program may use at most 128 MiB of HBM per device.

v0:
```python
import jax
import jax.numpy as jnp
from jax import lax
from jax.sharding import PartitionSpec as P

EPS = 1e-06


def shifted(value, axis, steps):
    count = lax.axis_size(axis)
    pairs = [(source, (source + steps) % count) for source in range(count)]
    return lax.ppermute(value, axis, pairs)


def matmul(left, right):
    return jnp.dot(left, right, preferred_element_type=jnp.float32)


def matmul_nt(left, right):
    return lax.dot_general(
        left, right, (((1,), (1,)), ((), ())), preferred_element_type=jnp.float32
    )


def matmul_tn(left, right):
    return lax.dot_general(
        left, right, (((0,), (0,)), ((), ())), preferred_element_type=jnp.float32
    )


def unit_parts(raw, raw_rate):
    values = raw.astype(jnp.float32)
    tangent = raw_rate.astype(jnp.float32)
    radius = jnp.sqrt(jnp.sum(values * values, axis=1, keepdims=True) + EPS)
    unit = values / radius
    rate = jnp.sum(unit * tangent, axis=1, keepdims=True)
    unit_tangent = (tangent - unit * rate) / radius
    return (unit, unit_tangent, radius, rate)


def unit_backward(unit, unit_tangent, radius, rate, grad, grad_rate):
    inner = jnp.sum(unit * grad, axis=1, keepdims=True)
    inner_rate = jnp.sum(unit_tangent * grad + unit * grad_rate, axis=1, keepdims=True)
    first = (grad - unit * inner) / radius
    return (grad_rate - unit_tangent * inner - unit * inner_rate - first * rate) / radius


def local(
    picture_averaged_encodings,
    caption_averaged_encodings,
    picture_mapping_matrix,
    caption_mapping_matrix,
    picture_weight_perturbation,
    caption_weight_perturbation,
    sharpness_multiplier,
    offset_additive,
):
    similarity_multiplier = sharpness_multiplier[0]
    logit_bias = offset_additive[0]
    tensor_rank = lax.axis_index("tensor")
    data_rank = lax.axis_index("dp")
    data_count = lax.axis_size("dp")
    image_cols = matmul(picture_averaged_encodings, picture_mapping_matrix).astype(jnp.bfloat16)
    image_cols_rate = matmul(picture_averaged_encodings, picture_weight_perturbation).astype(
        jnp.bfloat16
    )
    text_cols = matmul(caption_averaged_encodings, caption_mapping_matrix).astype(jnp.bfloat16)
    text_cols_rate = matmul(caption_averaged_encodings, caption_weight_perturbation).astype(
        jnp.bfloat16
    )
    image_raw, image_raw_rate = (
        lax.all_gather(image_cols, "tensor", axis=1, tiled=True),
        lax.all_gather(image_cols_rate, "tensor", axis=1, tiled=True),
    )
    text_raw, text_raw_rate = (
        lax.all_to_all(text_cols, "tensor", split_axis=0, concat_axis=1, tiled=True),
        lax.all_to_all(text_cols_rate, "tensor", split_axis=0, concat_axis=1, tiled=True),
    )
    image_unit, image_tangent, image_radius, image_rate = unit_parts(image_raw, image_raw_rate)
    text_unit, text_tangent, text_radius, text_rate = unit_parts(text_raw, text_raw_rate)
    image_half = image_unit.astype(jnp.bfloat16)
    image_tangent_half = image_tangent.astype(jnp.bfloat16)
    text_half = text_unit.astype(jnp.bfloat16)
    text_tangent_half = text_tangent.astype(jnp.bfloat16)
    image_rows = image_unit.shape[0]
    text_rows = text_unit.shape[0]
    image_ids = lax.broadcasted_iota(jnp.int32, (1, image_rows), 1)

    def block_terms(block_unit, block_tangent, positive):
        logits = similarity_multiplier * matmul_nt(block_unit, image_half) + logit_bias
        logit_rate = similarity_multiplier * (
            matmul_nt(block_unit, image_tangent_half) + matmul_nt(block_tangent, image_half)
        )
        probability = jax.nn.sigmoid(logits)
        weight = (probability - positive).astype(jnp.bfloat16)
        weight_rate = (probability * (1.0 - probability) * logit_rate).astype(jnp.bfloat16)
        text_term = similarity_multiplier * matmul(weight, image_half)
        text_term_rate = similarity_multiplier * (
            matmul(weight_rate, image_half) + matmul(weight, image_tangent_half)
        )
        image_term = similarity_multiplier * matmul_tn(weight, block_unit)
        image_term_rate = similarity_multiplier * (
            matmul_tn(weight_rate, block_unit) + matmul_tn(weight, block_tangent)
        )
        return (image_term, image_term_rate, text_term, text_term_rate)

    text_ids = lax.broadcasted_iota(jnp.int32, (text_rows, 1), 0) + tensor_rank * text_rows

    def hop(hop_index, carry):
        block_unit, block_tangent, block_grad, block_grad_rate, image_grad, image_grad_rate = carry
        source = (data_rank - hop_index) % data_count
        positive = ((text_ids == image_ids) & (source == data_rank)).astype(jnp.float32)
        image_term, image_term_rate, text_term, text_term_rate = block_terms(
            block_unit, block_tangent, positive
        )
        image_grad = image_grad + image_term
        image_grad_rate = image_grad_rate + image_term_rate
        block_grad = block_grad + text_term
        block_grad_rate = block_grad_rate + text_term_rate
        block_unit, block_tangent = shifted((block_unit, block_tangent), "dp", 1)
        block_grad, block_grad_rate = shifted((block_grad, block_grad_rate), "dp", 1)
        return (block_unit, block_tangent, block_grad, block_grad_rate, image_grad, image_grad_rate)

    text_empty = jnp.zeros(text_unit.shape, jnp.float32)
    image_empty = jnp.zeros(image_unit.shape, jnp.float32)
    start_state = (text_half, text_tangent_half, text_empty, text_empty, image_empty, image_empty)
    final_state = lax.fori_loop(0, data_count, hop, start_state)
    text_grad = final_state[2]
    text_grad_rate = final_state[3]
    image_grad = final_state[4]
    image_grad_rate = final_state[5]
    grad_cols, grad_rate_cols = (
        lax.psum_scatter(image_grad, "tensor", scatter_dimension=1, tiled=True),
        lax.psum_scatter(image_grad_rate, "tensor", scatter_dimension=1, tiled=True),
    )
    col_width = grad_cols.shape[1]
    col_start = tensor_rank * col_width
    unit_cols = lax.dynamic_slice_in_dim(image_unit, col_start, col_width, 1)
    tangent_cols = lax.dynamic_slice_in_dim(image_tangent, col_start, col_width, 1)
    inner_part = jnp.sum(unit_cols * grad_cols, axis=1, keepdims=True)
    inner_rate_part = jnp.sum(
        tangent_cols * grad_cols + unit_cols * grad_rate_cols, axis=1, keepdims=True
    )
    inner, inner_rate = lax.psum((inner_part, inner_rate_part), "tensor")
    first = (grad_cols - unit_cols * inner) / image_radius
    image_back = (
        grad_rate_cols - tangent_cols * inner - unit_cols * inner_rate - first * image_rate
    ) / image_radius
    image_back_half = image_back.astype(jnp.bfloat16)
    text_back_half = unit_backward(
        text_unit, text_tangent, text_radius, text_rate, text_grad, text_grad_rate
    ).astype(jnp.bfloat16)
    text_back_cols = lax.all_to_all(
        text_back_half, "tensor", split_axis=1, concat_axis=0, tiled=True
    )
    image_terms = matmul_tn(picture_averaged_encodings, image_back_half)
    text_terms_head = matmul_tn(caption_averaged_encodings, text_back_cols)
    image_hvp, text_hvp = (
        lax.psum_scatter(image_terms, "dp", scatter_dimension=0, tiled=True),
        lax.psum_scatter(text_terms_head, "dp", scatter_dimension=0, tiled=True),
    )
    return (image_hvp, text_hvp)


def solution(mesh):
    in_specs = (
        P("dp", None),
        P("dp", None),
        P(None, "tensor"),
        P(None, "tensor"),
        P(None, "tensor"),
        P(None, "tensor"),
        P(),
        P(),
    )
    out_specs = (P("dp", "tensor"), P("dp", "tensor"))
    return jax.shard_map(local, mesh=mesh, in_specs=in_specs, out_specs=out_specs, check_vma=False)
```

profile of v0, /device:TPU:1, one launch (start us, length us, event | category | flops | bytes accessed | tf_op | source)
XLA Modules:
  0.0 1069.6 jit_solution(12950343320937254315)
XLA Ops:
  14.8 6.8 all-to-all-start
  32.6 6.9 all-to-all-done.1
  41.1 10.7 all-gather.3.cloned.1.call-done
  53.8 35.7 %all-gather.5.cloned.1.call-done = bf16[768,1152]{0,1:T(8,128)(2,1)} async-done(((bf16[768,72]{0,1:T(8,128)(2,1)}), bf16[768,1152]{0,1:T(8,128)(2,1)}) %all-gather.5.cloned.1.call-update) | async-done | bytes 1769488 | tf_op jit(solution)/shard_map/all_gather | solution.py:73
  105.6 611.7 %while.26 = (s32[]{:T(128)}, bf16[48,1152]{1,0:T(8,128)(2,1)}, bf16[48,1152]{1,0:T(8,128)(2,1)}, f32[48,1152]{1,0:T(8,128)}, f32[48,1152]{1,0:T(8,128)}, /*index...) while((s32[]{:T(128)}, bf16[48,1152]{1,0:T(8,128)(2,1)}, ...), condition=%wide.region_5.6_spmd.clone, body=%wide.region_4.5_spmd.clone.sunk | while | flops 771471424 | bytes 45786044 | solution.py:127
  171.3 6.4 fusion.117
  208.7 6.4 fusion.117
  245.5 6.4 fusion.117
  284.4 6.4 fusion.117
  324.8 6.4 fusion.117
  362.1 6.4 fusion.117
  398.9 6.4 fusion.117
  437.8 6.4 fusion.117
  478.2 6.4 fusion.117
  515.5 6.4 fusion.117
  552.3 6.4 fusion.117
  669.0 6.4 fusion.117
  705.7 6.4 fusion.117
  735.1 22.0 %all-to-all-start.2 = ((bf16[48,16,72]{2,0,1:T(8,128)(2,1)}), bf16[48,16,72]{2,0,1:T(8,128)(2,1)}, u32[]{:S(2)}, u32[]{:S(2)}) async-start(bf16[48,16,72]{2,0,1:T(8,128)(2,1)} %copy.46), calls=%async_computation.4 | async-start | bytes 393216 | tf_op jit(solution)/shard_map/all_to_all | solution.py:153
  757.2 7.0 all-to-all-done.2
  766.2 40.5 %reduce-scatter.5.cloned.1.call-done = f32[768,72]{0,1:T(8,128)} async-done(((f32[768,1152]{0,1:T(8,128)}), f32[768,72]{0,1:T(8,128)}) %reduce-scatter.5.cloned.1.call-update) | async-done | bytes 221200 | tf_op jit(solution)/shard_map/reduce_scatter | solution.py:134
  806.7 70.6 %reduce-scatter.7.cloned.1.call-done = f32[768,72]{0,1:T(8,128)} async-done(((f32[768,1152]{0,1:T(8,128)}), f32[768,72]{0,1:T(8,128)}) %reduce-scatter.7.cloned.1.call-update) | async-done | bytes 221200 | tf_op jit(solution)/shard_map/reduce_scatter | solution.py:133
  878.6 31.5 %all-reduce.2 = (f32[768]{0:T(1024)}, f32[768]{0:T(1024)}) all-reduce(f32[768]{0:T(1024)S(1)} %get-tuple-element.448, f32[768]{0:T(1024)S(1)} %get-tuple-element.447), channel_id=1, replica_groups=mesh['dp'=16,'tensor'=16] {'tensor'}, use_global_device_ids=true, to_apply=%region_11.12 | all-reduce | flops 1536 | bytes 12288 | tf_op jit(solution)/shard_map/psum | solution.py:144
  913.8 146.8 %all-reduce.6.cloned.1.call-done = (f32[1152,72]{0,1:T(8,128)}, f32[1152,72]{0,1:T(8,128)}) async-done(((f32[1152,72]{0,1:T(8,128)}, f32[1152,72]{0,1:T(8,128)}), (f32[1152,72]{0,1:T(8,128)}, f32[1152,72]{0,1:T(8,128)})) %all-reduce.6.cloned.1.call-update) | async-done | bytes 663568
  (472 shorter events, 592.5 us)
Async XLA Ops:
  7.2 44.6 %all-gather.3.cloned.1.call-start = ((), (), s32[]{:S(2)}) async-start(), calls=%async_computation.5 | async-start | bytes 1880064 | tf_op jit(solution)/shard_map/all_gather | solution.py:72
  10.3 79.1 %all-gather.5.cloned.1.call-start = ((), (), s32[]{:S(2)}) async-start(), calls=%async_computation.6 | async-start | bytes 1880064 | tf_op jit(solution)/shard_map/all_gather | solution.py:73
  32.2 774.5 %reduce-scatter.5.cloned.1.call-start = ((), (), s32[]{:S(2)}) async-start(), calls=%async_computation.7 | async-start | bytes 3760128 | tf_op jit(solution)/shard_map/reduce_scatter | solution.py:134
  107.2 35.4 %collective-permute-start = (bf16[48,1152]{1,0:T(8,128)(2,1)}, bf16[48,1152]{1,0:T(8,128)(2,1)}, u32[]{:S(2)}, u32[]{:S(2)}) collective-permute-start(bf16[48,1152]{1,0:T(8,128)(2,1)} %copy.61), channel_id=1, source_target_pairs={{0,16},{16,32},{32,48},{48,64},{64,80},{80,96},{96,112},{112,128},... | collective-permute-start | bytes 331784 | tf_op jit(solution)/shard_map/while/body/eval_jaxpr/ppermute | solution.py:12
  144.2 38.8 %collective-permute-start = (bf16[48,1152]{1,0:T(8,128)(2,1)}, bf16[48,1152]{1,0:T(8,128)(2,1)}, u32[]{:S(2)}, u32[]{:S(2)}) collective-permute-start(bf16[48,1152]{1,0:T(8,128)(2,1)} %copy.61), channel_id=1, source_target_pairs={{0,16},{16,32},{32,48},{48,64},{64,80},{80,96},{96,112},{112,128},... | collective-permute-start | bytes 331784 | tf_op jit(solution)/shard_map/while/body/eval_jaxpr/ppermute | solution.py:12
  184.5 35.8 %collective-permute-start = (bf16[48,1152]{1,0:T(8,128)(2,1)}, bf16[48,1152]{1,0:T(8,128)(2,1)}, u32[]{:S(2)}, u32[]{:S(2)}) collective-permute-start(bf16[48,1152]{1,0:T(8,128)(2,1)} %copy.61), channel_id=1, source_target_pairs={{0,16},{16,32},{32,48},{48,64},{64,80},{80,96},{96,112},{112,128},... | collective-permute-start | bytes 331784 | tf_op jit(solution)/shard_map/while/body/eval_jaxpr/ppermute | solution.py:12
  221.9 35.2 %collective-permute-start = (bf16[48,1152]{1,0:T(8,128)(2,1)}, bf16[48,1152]{1,0:T(8,128)(2,1)}, u32[]{:S(2)}, u32[]{:S(2)}) collective-permute-start(bf16[48,1152]{1,0:T(8,128)(2,1)} %copy.61), channel_id=1, source_target_pairs={{0,16},{16,32},{32,48},{48,64},{64,80},{80,96},{96,112},{112,128},... | collective-permute-start | bytes 331784 | tf_op jit(solution)/shard_map/while/body/eval_jaxpr/ppermute | solution.py:12
  258.6 37.4 %collective-permute-start = (bf16[48,1152]{1,0:T(8,128)(2,1)}, bf16[48,1152]{1,0:T(8,128)(2,1)}, u32[]{:S(2)}, u32[]{:S(2)}) collective-permute-start(bf16[48,1152]{1,0:T(8,128)(2,1)} %copy.61), channel_id=1, source_target_pairs={{0,16},{16,32},{32,48},{48,64},{64,80},{80,96},{96,112},{112,128},... | collective-permute-start | bytes 331784 | tf_op jit(solution)/shard_map/while/body/eval_jaxpr/ppermute | solution.py:12
  297.6 38.8 %collective-permute-start = (bf16[48,1152]{1,0:T(8,128)(2,1)}, bf16[48,1152]{1,0:T(8,128)(2,1)}, u32[]{:S(2)}, u32[]{:S(2)}) collective-permute-start(bf16[48,1152]{1,0:T(8,128)(2,1)} %copy.61), channel_id=1, source_target_pairs={{0,16},{16,32},{32,48},{48,64},{64,80},{80,96},{96,112},{112,128},... | collective-permute-start | bytes 331784 | tf_op jit(solution)/shard_map/while/body/eval_jaxpr/ppermute | solution.py:12
  301.6 34.7 %collective-permute-start.1 = (bf16[48,1152]{1,0:T(8,128)(2,1)}, bf16[48,1152]{1,0:T(8,128)(2,1)}, u32[]{:S(2)}, u32[]{:S(2)}) collective-permute-start(bf16[48,1152]{1,0:T(8,128)(2,1)} %copy.62), channel_id=1, source_target_pairs={{0,16},{16,32},{32,48},{48,64},{64,80},{80,96},{96,112},{112,128},... | collective-permute-start | bytes 331784 | tf_op jit(solution)/shard_map/while/body/eval_jaxpr/ppermute | solution.py:12
  337.9 35.8 %collective-permute-start = (bf16[48,1152]{1,0:T(8,128)(2,1)}, bf16[48,1152]{1,0:T(8,128)(2,1)}, u32[]{:S(2)}, u32[]{:S(2)}) collective-permute-start(bf16[48,1152]{1,0:T(8,128)(2,1)} %copy.61), channel_id=1, source_target_pairs={{0,16},{16,32},{32,48},{48,64},{64,80},{80,96},{96,112},{112,128},... | collective-permute-start | bytes 331784 | tf_op jit(solution)/shard_map/while/body/eval_jaxpr/ppermute | solution.py:12
  375.3 35.2 %collective-permute-start = (bf16[48,1152]{1,0:T(8,128)(2,1)}, bf16[48,1152]{1,0:T(8,128)(2,1)}, u32[]{:S(2)}, u32[]{:S(2)}) collective-permute-start(bf16[48,1152]{1,0:T(8,128)(2,1)} %copy.61), channel_id=1, source_target_pairs={{0,16},{16,32},{32,48},{48,64},{64,80},{80,96},{96,112},{112,128},... | collective-permute-start | bytes 331784 | tf_op jit(solution)/shard_map/while/body/eval_jaxpr/ppermute | solution.py:12
  412.1 37.4 %collective-permute-start = (bf16[48,1152]{1,0:T(8,128)(2,1)}, bf16[48,1152]{1,0:T(8,128)(2,1)}, u32[]{:S(2)}, u32[]{:S(2)}) collective-permute-start(bf16[48,1152]{1,0:T(8,128)(2,1)} %copy.61), channel_id=1, source_target_pairs={{0,16},{16,32},{32,48},{48,64},{64,80},{80,96},{96,112},{112,128},... | collective-permute-start | bytes 331784 | tf_op jit(solution)/shard_map/while/body/eval_jaxpr/ppermute | solution.py:12
  451.0 38.8 %collective-permute-start = (bf16[48,1152]{1,0:T(8,128)(2,1)}, bf16[48,1152]{1,0:T(8,128)(2,1)}, u32[]{:S(2)}, u32[]{:S(2)}) collective-permute-start(bf16[48,1152]{1,0:T(8,128)(2,1)} %copy.61), channel_id=1, source_target_pairs={{0,16},{16,32},{32,48},{48,64},{64,80},{80,96},{96,112},{112,128},... | collective-permute-start | bytes 331784 | tf_op jit(solution)/shard_map/while/body/eval_jaxpr/ppermute | solution.py:12
  455.1 34.7 %collective-permute-start.1 = (bf16[48,1152]{1,0:T(8,128)(2,1)}, bf16[48,1152]{1,0:T(8,128)(2,1)}, u32[]{:S(2)}, u32[]{:S(2)}) collective-permute-start(bf16[48,1152]{1,0:T(8,128)(2,1)} %copy.62), channel_id=1, source_target_pairs={{0,16},{16,32},{32,48},{48,64},{64,80},{80,96},{96,112},{112,128},... | collective-permute-start | bytes 331784 | tf_op jit(solution)/shard_map/while/body/eval_jaxpr/ppermute | solution.py:12
  491.4 35.8 %collective-permute-start = (bf16[48,1152]{1,0:T(8,128)(2,1)}, bf16[48,1152]{1,0:T(8,128)(2,1)}, u32[]{:S(2)}, u32[]{:S(2)}) collective-permute-start(bf16[48,1152]{1,0:T(8,128)(2,1)} %copy.61), channel_id=1, source_target_pairs={{0,16},{16,32},{32,48},{48,64},{64,80},{80,96},{96,112},{112,128},... | collective-permute-start | bytes 331784 | tf_op jit(solution)/shard_map/while/body/eval_jaxpr/ppermute | solution.py:12
  528.7 35.2 %collective-permute-start = (bf16[48,1152]{1,0:T(8,128)(2,1)}, bf16[48,1152]{1,0:T(8,128)(2,1)}, u32[]{:S(2)}, u32[]{:S(2)}) collective-permute-start(bf16[48,1152]{1,0:T(8,128)(2,1)} %copy.61), channel_id=1, source_target_pairs={{0,16},{16,32},{32,48},{48,64},{64,80},{80,96},{96,112},{112,128},... | collective-permute-start | bytes 331784 | tf_op jit(solution)/shard_map/while/body/eval_jaxpr/ppermute | solution.py:12
  565.5 37.4 %collective-permute-start = (bf16[48,1152]{1,0:T(8,128)(2,1)}, bf16[48,1152]{1,0:T(8,128)(2,1)}, u32[]{:S(2)}, u32[]{:S(2)}) collective-permute-start(bf16[48,1152]{1,0:T(8,128)(2,1)} %copy.61), channel_id=1, source_target_pairs={{0,16},{16,32},{32,48},{48,64},{64,80},{80,96},{96,112},{112,128},... | collective-permute-start | bytes 331784 | tf_op jit(solution)/shard_map/while/body/eval_jaxpr/ppermute | solution.py:12
  604.5 38.8 %collective-permute-start = (bf16[48,1152]{1,0:T(8,128)(2,1)}, bf16[48,1152]{1,0:T(8,128)(2,1)}, u32[]{:S(2)}, u32[]{:S(2)}) collective-permute-start(bf16[48,1152]{1,0:T(8,128)(2,1)} %copy.61), channel_id=1, source_target_pairs={{0,16},{16,32},{32,48},{48,64},{64,80},{80,96},{96,112},{112,128},... | collective-permute-start | bytes 331784 | tf_op jit(solution)/shard_map/while/body/eval_jaxpr/ppermute | solution.py:12
  608.5 34.7 %collective-permute-start.1 = (bf16[48,1152]{1,0:T(8,128)(2,1)}, bf16[48,1152]{1,0:T(8,128)(2,1)}, u32[]{:S(2)}, u32[]{:S(2)}) collective-permute-start(bf16[48,1152]{1,0:T(8,128)(2,1)} %copy.62), channel_id=1, source_target_pairs={{0,16},{16,32},{32,48},{48,64},{64,80},{80,96},{96,112},{112,128},... | collective-permute-start | bytes 331784 | tf_op jit(solution)/shard_map/while/body/eval_jaxpr/ppermute | solution.py:12
  644.8 35.8 %collective-permute-start = (bf16[48,1152]{1,0:T(8,128)(2,1)}, bf16[48,1152]{1,0:T(8,128)(2,1)}, u32[]{:S(2)}, u32[]{:S(2)}) collective-permute-start(bf16[48,1152]{1,0:T(8,128)(2,1)} %copy.61), channel_id=1, source_target_pairs={{0,16},{16,32},{32,48},{48,64},{64,80},{80,96},{96,112},{112,128},... | collective-permute-start | bytes 331784 | tf_op jit(solution)/shard_map/while/body/eval_jaxpr/ppermute | solution.py:12
  682.1 35.2 %collective-permute-start = (bf16[48,1152]{1,0:T(8,128)(2,1)}, bf16[48,1152]{1,0:T(8,128)(2,1)}, u32[]{:S(2)}, u32[]{:S(2)}) collective-permute-start(bf16[48,1152]{1,0:T(8,128)(2,1)} %copy.61), channel_id=1, source_target_pairs={{0,16},{16,32},{32,48},{48,64},{64,80},{80,96},{96,112},{112,128},... | collective-permute-start | bytes 331784 | tf_op jit(solution)/shard_map/while/body/eval_jaxpr/ppermute | solution.py:12
  722.6 154.8 %reduce-scatter.7.cloned.1.call-start = ((), (), s32[]{:S(2)}) async-start(), calls=%async_computation.8 | async-start | bytes 3760128 | tf_op jit(solution)/shard_map/reduce_scatter | solution.py:133
  757.1 303.5 %all-reduce.6.cloned.1.call-start = ((), (), s32[]{:S(2)}) async-start(), calls=%async_computation.9 | async-start | bytes 1327104
  (105 other events, 1717.1 us)
Sparse Core Ops, SparseCore 0:
  10.4 41.3 all-gather.2
  53.7 35.6 all-gather.4
  722.7 83.9 reduce-scatter.4
  809.1 68.1 reduce-scatter.6
  912.7 147.8 all-reduce.5
where the time goes:
time: 1090 us; the launch traced here: 1070 us
  matrix products  458 us (42%)
  waiting for transfers between devices  323 us (30%)
  starting transfers between devices  147 us (13%)
  local copies, waits for them, and re-layouts  77.3 us (7%)
  blocking collectives  31.5 us (3%)
  other arithmetic  16.5 us (2%)
  between operations  14.6 us (1%)
    dot_general x50, matrix products, matmul_tn(): lax.dot_general(left, right, (((0,), (0,)), ((), ())), preferred_element_...  241 us
    unnamed x6, waiting for transfers between devices  147 us
    dot_general x48, matrix products, matmul_nt(): lax.dot_general(left, right, (((1,), (1,)), ((), ())), preferred_element_...  116 us
    ppermute x64, starting transfers between devices, shifted(): return lax.ppermute(value, axis, pairs)  114 us
    dot_general x52, matrix products, matmul(): return jnp.dot(left, right, preferred_element_type=jnp.float32)  101 us
    reduce_scatter x1, waiting for transfers between devices, local(): lax.psum_scatter(image_grad, 'tensor', scatter_dimension=1, tiled=True)  70.6 us
    while x128, local copies, waits for them, and re-layouts  50.1 us
    reduce_scatter x1, waiting for transfers between devices, local(): lax.psum_scatter(image_grad_rate, 'tensor', scatter_dimension=1, tiled=True)  40.5 us
  transfers between devices with their start and end apart: 72, of which 8 were waited for; matrix products, arithmetic and copies ran while one was open for 46% of the time, Pallas kernels for 0%

commit v1 on v0

v1 whole, which is shorter than its diff:
```python
import functools

import jax
import jax.numpy as jnp
from jax import lax
from jax.experimental import pallas as pl
from jax.experimental.pallas import tpu as pltpu
from jax.sharding import PartitionSpec as P

EPS = 1e-06
MESH = pl.DeviceIdType.MESH
F32 = jnp.float32
BF16 = jnp.bfloat16

DP_SLOTS = (
    (True, 0), (False, 0), (True, 1), (True, -1),
    (False, 1), (False, -1), (True, 2), (True, -2),
    (False, 2), (False, -2), (True, 3), (True, -3),
    (False, 3), (False, -3), (True, 4), (False, -4),
)
TP_CHIPS = (
    (True, 0), (False, 0), (True, 1), (True, -1),
    (False, 1), (False, -1), (True, 2), (False, -2),
)
TP_SLOTS = tuple((y, x, c) for y, x in TP_CHIPS for c in (True, False))


def mirror(slots, period):
    found = []
    for slot in slots:
        back = (slot[0], -slot[1]) + tuple(slot[2:])
        if back not in slots:
            back = (slot[0], slot[1]) + tuple(slot[2:])
            assert 2 * abs(slot[1]) == period
        found.append(slots.index(back))
    return tuple(found)


def dot_nn(a, b):
    return lax.dot_general(a, b, (((1,), (0,)), ((), ())), preferred_element_type=F32)


def dot_nt(a, b):
    return lax.dot_general(a, b, (((1,), (1,)), ((), ())), preferred_element_type=F32)


def dot_tn(a, b):
    return lax.dot_general(a, b, (((0,), (0,)), ((), ())), preferred_element_type=F32)


def split_hi(value):
    hi = value.astype(BF16)
    lo = (value - hi.astype(F32)).astype(BF16)
    return hi, lo


def lanes_of(values, rows):
    lane = lax.broadcasted_iota(jnp.int32, (rows, 128), 1)
    out = jnp.zeros((rows, 128), F32)
    for index, value in enumerate(values):
        out = jnp.where(lane == index, value.astype(F32), out)
    return out


def kernel(
    nz, nx, D, W,
    enc_i, enc_t, w_i, w_t, dw_i, dw_t, scalars,
    out_i, out_t,
    wpad, x_buf, x_got, raw, img, txt, gi, pb_buf, at_buf, csum,
    si_buf, st_buf, ri_buf, rt_buf, stage, cols, hv, hv_got,
    fs, fr, ais, air, ats, atr, ris, rir, rts, rtr, bs, br, hs, hr,
):
    dp = lax.axis_index("dp")
    tp = lax.axis_index("tensor")
    z, h = dp // 2, dp % 2
    y, x, c = tp // (2 * nx), (tp // 2) % nx, tp % 2
    rows = enc_i.shape[0]
    share = rows // 16
    DX = D + 128
    DE = 2 * D + 128
    s = scalars[0]
    bias = scalars[1]

    def dp_of(slot):
        same, back = slot
        zz = (z - back + nz) % nz
        hh = h if same else 1 - h
        return zz * 2 + hh

    def tp_of(slot):
        same, back, own = slot
        xx = (x - back + nx) % nx
        yy = y if same else 1 - y
        cc = c if own else 1 - c
        return (yy * nx + xx) * 2 + cc

    dp_ids = [dp_of(q) for q in DP_SLOTS]
    tp_ids = [tp_of(q) for q in TP_SLOTS]
    dp_back = mirror(DP_SLOTS, nz)
    tp_back = mirror(TP_SLOTS, nx)
    d_at = {q: i for i, q in enumerate(DP_SLOTS)}
    t_at = {q: i for i, q in enumerate(TP_SLOTS)}

    started = []

    def send(src, dst, ssem, rsem, device):
        copy = pltpu.make_async_remote_copy(
            src_ref=src, dst_ref=dst, send_sem=ssem, recv_sem=rsem,
            device_id=device, device_id_type=MESH,
        )
        copy.start()
        started.append(copy)

    def arrived(dst, rsem):
        pltpu.make_async_remote_copy(
            src_ref=dst, dst_ref=dst, send_sem=fs.at[0], recv_sem=rsem,
            device_id=(dp, tp), device_id_type=MESH,
        ).wait_recv()

    barrier = pltpu.get_barrier_semaphore()
    for q in range(1, 16):
        pl.semaphore_signal(barrier, inc=1, device_id=(dp_ids[q], tp), device_id_type=MESH)
        pl.semaphore_signal(barrier, inc=1, device_id=(dp, tp_ids[q]), device_id_type=MESH)

    wpad[...] = jnp.zeros_like(wpad)
    wpad[:, 0:W] = w_i[...]
    wpad[:, 128 : 128 + W] = dw_i[...]
    wpad[:, 256 : 256 + W] = w_t[...]
    wpad[:, 384 : 384 + W] = dw_t[...]

    def project(r, carry):
        at = pl.ds(pl.multiple_of(r * 256, 256), 256)
        x_buf[at, 0:256] = dot_nn(enc_i[at, :], wpad[:, 0:256]).astype(BF16)
        x_buf[at, 256:512] = dot_nn(enc_t[at, :], wpad[:, 256:512]).astype(BF16)
        return carry

    lax.fori_loop(0, rows // 256, project, 0)
    pl.semaphore_wait(barrier, 30)

    def share_at(index):
        return pl.ds(pl.multiple_of(index * share, share), share)

    for q in range(1, 16):
        send(x_buf.at[share_at(tp_ids[q]), :], x_got.at[tp], fs.at[q], fr.at[tp], (dp, tp_ids[q]))
    x_got[pl.ds(tp, 1)] = x_buf[share_at(tp), :].reshape(1, share, 512)
    for q in range(1, 16):
        arrived(x_got.at[tp_ids[q]], fr.at[tp_ids[q]])
    for q in range(16):
        for k in range(4):
            raw[k, :, q * W : (q + 1) * W] = x_got[q, :, k * 128 : k * 128 + W].astype(F32)

    def unit_parts(values, tangent):
        radius = jnp.sqrt(jnp.sum(values * values, axis=1, keepdims=True) + EPS)
        unit = values / radius
        rate = jnp.sum(unit * tangent, axis=1, keepdims=True)
        unit_tangent = (tangent - unit * rate) / radius
        return unit, unit_tangent, radius, rate / radius

    for k, buf in ((0, img), (2, txt)):
        unit, tangent, radius, ratio = unit_parts(raw[k], raw[k + 1])
        buf[0:share, 0:D] = unit.astype(BF16)
        buf[0:share, D : 2 * D] = tangent.astype(BF16)
        hi, lo = split_hi(ratio)
        buf[0:share, 2 * D : DE] = lanes_of((hi, lo), share).astype(BF16)

    def iat(slot):
        return img.at[pl.ds(slot * share, share), :]

    def tat(slot):
        return txt.at[pl.ds(slot * share, share), :]

    counts = {"i": 0, "t": 0}

    def isend(src, dst, device):
        send(iat(src), iat(dst), ais.at[counts["i"]], air.at[dst], (dp, device))
        counts["i"] += 1

    def tsend(src, dst, device):
        send(tat(src), tat(dst), ats.at[counts["t"]], atr.at[dst], (device, tp))
        counts["t"] += 1

    def iwait(slot):
        arrived(iat(slot), air.at[slot])

    def twait(slot):
        arrived(tat(slot), atr.at[slot])

    sib = tp_ids[t_at[(True, 0, False)]]
    x_right = tp_ids[t_at[(True, -1, True)]]
    x_left = tp_ids[t_at[(True, 1, True)]]
    z_right = dp_ids[d_at[(True, -1)]]
    z_left = dp_ids[d_at[(True, 1)]]

    def t_on(same, back):
        src = d_at[(same, back)]
        if back >= 0 and (same, back + 1) in d_at:
            tsend(src, d_at[(same, back + 1)], z_right)
        if back <= 0 and (same, back - 1) in d_at:
            tsend(src, d_at[(same, back - 1)], z_left)

    def i_on(same, back):
        src = t_at[(same, back, True)]
        if back >= 0 and (same, back + 1, True) in t_at:
            isend(src, t_at[(same, back + 1, True)], x_right)
        if back <= 0 and (same, back - 1, True) in t_at:
            isend(src, t_at[(same, back - 1, True)], x_left)
        isend(src, t_at[(same, back, False)], sib)

    def t_step(same, back):
        twait(d_at[(same, back)])
        t_on(same, back)

    def i_step(same, back):
        iwait(t_at[(same, back, True)])
        i_on(same, back)

    isend(0, t_at[(False, 0, True)], tp_ids[t_at[(False, 0, True)]])
    tsend(0, d_at[(False, 0)], dp_ids[d_at[(False, 0)]])
    i_on(True, 0)
    t_on(True, 0)
    i_step(False, 0)
    t_step(False, 0)
    for back in (1, -1):
        i_step(True, back)
        t_step(True, back)
    for back in (1, -1):
        i_step(False, back)
        t_step(False, back)
    i_step(True, 2)
    i_step(False, -2)
    t_step(True, 2)
    t_step(True, -2)
    for chip in TP_CHIPS:
        iwait(t_at[chip + (False,)])

    eye = lanes_of([(lax.broadcasted_iota(jnp.int32, (8, 1), 0) == k) for k in range(8)], 8).astype(BF16)
    TC = 4 * share
    RB = 256

    def chunk(ci):
        at = pl.ds(ci * TC, TC)
        ends = txt[at, 2 * D : DE].astype(F32)
        sigma = ends[:, 0:1] + ends[:, 1:2]
        csum[...] = jnp.zeros_like(csum)

        def block(r, carry):
            ra = pl.ds(pl.multiple_of(r * RB, RB), RB)
            tu = txt[at, 0:D]
            tt = txt[at, D : 2 * D]
            iu = img[ra, 0:D]
            it = img[ra, D : 2 * D]
            extra = img[ra, 2 * D : DE].astype(F32)
            rho = extra[:, 0:1] + extra[:, 1:2]
            cosine = dot_nt(iu, tu)
            cross = dot_nt(it, tu) + dot_nt(iu, tt)
            prob = jax.nn.sigmoid(s * cosine + bias)
            rate = prob * (1.0 - prob) * (s * cross)
            pb = prob.astype(BF16)
            q1 = prob * cosine
            q2 = prob * cross + rate * cosine
            csum[0:1, :] += jnp.sum(q1, axis=0, keepdims=True)
            csum[1:2, :] += jnp.sum(q2, axis=0, keepdims=True)
            rb = rate.astype(BF16)
            pb_buf[ra, :] = pb
            at_buf[ra, :] = rb
            gain = dot_nn(rb, tu) + dot_nn(pb, tt) - rho * dot_nn(pb, tu)
            sums = lanes_of((jnp.sum(q1, axis=1, keepdims=True), jnp.sum(q2, axis=1, keepdims=True)), RB)
            if ci == 0:
                gi[ra, 0:D] = gain
                gi[ra, D:DX] = sums
            else:
                gi[ra, 0:D] += gain
                gi[ra, D:DX] += sums
            return carry

        lax.fori_loop(0, rows // RB, block, 0)

        hi, lo = split_hi(csum[...])
        tops = jnp.concatenate([hi[0:2].astype(F32), lo[0:2].astype(F32), jnp.zeros((4, TC), F32)], axis=0)
        st_buf[at, D:DX] = dot_tn(tops.astype(BF16), eye).astype(BF16)

        def columns(k, carry):
            ka = pl.ds(pl.multiple_of(k * 384, 128), 384)
            kb = pl.ds(pl.multiple_of(D + k * 384, 128), 384)
            gain = dot_tn(at_buf[...], img[:, ka]) + dot_tn(pb_buf[...], img[:, kb])
            st_buf[at, ka] = (gain - sigma * dot_tn(pb_buf[...], img[:, ka])).astype(BF16)
            return carry

        lax.fori_loop(0, D // 384, columns, 0)
        for q in range(4 * ci, 4 * ci + 4):
            if q > 0:
                k = dp_back[q]
                send(st_buf.at[pl.ds(q * share, share), :], rt_buf.at[k], rts.at[q], rtr.at[k], (dp_ids[q], tp))

    chunk(0)
    for back in (2, -2):
        t_step(False, back)
    t_step(True, 3)
    t_step(True, -3)
    chunk(1)
    t_step(False, -3)
    t_step(False, 3)
    chunk(2)
    t_step(True, 4)
    t_step(False, -4)
    chunk(3)

    for q in range(1, 16):
        qa = pl.ds(q * share, share)
        si_buf[qa, 0:D] = gi[qa, 0:D].astype(BF16)
        hi, lo = split_hi(gi[qa, D:DX])
        hi, lo = hi.astype(F32), lo.astype(F32)
        si_buf[qa, D:DX] = lanes_of((hi[:, 0:1], hi[:, 1:2], lo[:, 0:1], lo[:, 1:2]), share).astype(BF16)
        k = tp_back[q]
        send(si_buf.at[qa, :], ri_buf.at[k], ris.at[q], rir.at[k], (dp, tp_ids[q]))

    for q in range(1, 16):
        arrived(rt_buf.at[q], rtr.at[q])
    for q in range(1, 16):
        arrived(ri_buf.at[q], rir.at[q])

    iu, it = img[0:share, 0:D].astype(F32), img[0:share, D : 2 * D].astype(F32)
    tu, tt = txt[0:share, 0:D].astype(F32), txt[0:share, D : 2 * D].astype(F32)
    pair_cos = jnp.sum(iu * tu, axis=1, keepdims=True)
    pair_cross = jnp.sum(it * tu + iu * tt, axis=1, keepdims=True)
    stage[...] = jnp.zeros_like(stage)
    for k, got in ((0, ri_buf), (1, rt_buf)):
        if k == 0:
            total = gi[0:share, 0:D]
            inner = gi[0:share, D : D + 1]
            inner_rate = gi[0:share, D + 1 : D + 2]
            other, other_tangent = tu, tt
        else:
            total = st_buf[0:share, 0:D].astype(F32)
            own = st_buf[0:share, D:DX].astype(F32)
            inner = own[:, 0:1] + own[:, 2:3]
            inner_rate = own[:, 1:2] + own[:, 3:4]
            other, other_tangent = iu, it
        for q in range(1, 16):
            total = total + got[q, :, 0:D].astype(F32)
            ends = got[q, :, D:DX].astype(F32)
            inner = inner + (ends[:, 0:1] + ends[:, 2:3])
            inner_rate = inner_rate + (ends[:, 1:2] + ends[:, 3:4])
        unit, tangent, radius, ratio = unit_parts(raw[2 * k], raw[2 * k + 1])
        total = s * (total + (ratio * other - other_tangent))
        inner = s * (inner - pair_cos)
        inner_rate = s * (inner_rate - pair_cross)
        raw[2 * k] = (total - tangent * inner - unit * (inner_rate - ratio * inner)) / radius
        for q in range(16):
            hi, lo = split_hi(raw[2 * k, :, q * W : (q + 1) * W])
            stage[q, :, k * 256 : k * 256 + W] = hi
            stage[q, :, k * 256 + 128 : k * 256 + 128 + W] = lo

    for q in range(1, 16):
        send(stage.at[tp_ids[q]], cols.at[share_at(tp), :], bs.at[q], br.at[tp], (dp, tp_ids[q]))
    cols[share_at(tp), :] = stage[pl.ds(tp, 1)].reshape(share, 512)
    for q in range(1, 16):
        arrived(cols.at[share_at(tp_ids[q]), :], br.at[tp_ids[q]])

    def head(k, carry):
        ka = pl.ds(pl.multiple_of(k * 128, 128), 128)
        both = dot_tn(enc_i[:, ka], cols[:, 0:256])
        hv[ka, 0:128] = both[:, 0:128] + both[:, 128:256]
        both = dot_tn(enc_t[:, ka], cols[:, 256:512])
        hv[ka, 128:256] = both[:, 0:128] + both[:, 128:256]
        return carry

    lax.fori_loop(0, D // 128, head, 0)

    def own_rows(index):
        return pl.ds(pl.multiple_of(index * W, 8), W)

    for q in range(1, 16):
        k = dp_back[q]
        send(hv.at[own_rows(dp_ids[q]), :], hv_got.at[k], hs.at[q], hr.at[k], (dp_ids[q], tp))
    total = hv[own_rows(dp), :]
    for q in range(1, 16):
        arrived(hv_got.at[q], hr.at[q])
        total = total + hv_got[q]
    out_i[...] = total[:, 0:W]
    out_t[...] = total[:, 128 : 128 + W]
    for copy in started:
        copy.wait_send()


def solution(mesh):
    nz = mesh.shape["dp"] // 2
    nx = mesh.shape["tensor"] // 4

    def local(enc_i, enc_t, w_i, w_t, dw_i, dw_t, sharpness, offset):
        rows, D = enc_i.shape
        W = w_i.shape[1]
        share = rows // 16
        DX, DE = D + 128, 2 * D + 128
        scalars = jnp.concatenate([sharpness, offset])
        vmem = pl.BlockSpec(memory_space=pltpu.VMEM)
        sem = pltpu.SemaphoreType.DMA((16,))
        return pl.pallas_call(
            functools.partial(kernel, nz, nx, D, W),
            out_shape=[jax.ShapeDtypeStruct((W, W), F32)] * 2,
            in_specs=[vmem] * 6 + [pl.BlockSpec(memory_space=pltpu.SMEM)],
            out_specs=[vmem] * 2,
            scratch_shapes=[
                pltpu.VMEM((D, 512), BF16),
                pltpu.VMEM((rows, 512), BF16),
                pltpu.VMEM((16, share, 512), BF16),
                pltpu.VMEM((4, share, D), F32),
                pltpu.VMEM((rows, DE), BF16),
                pltpu.VMEM((rows, DE), BF16),
                pltpu.VMEM((rows, DX), F32),
                pltpu.VMEM((rows, 4 * share), BF16),
                pltpu.VMEM((rows, 4 * share), BF16),
                pltpu.VMEM((8, 4 * share), F32),
                pltpu.VMEM((rows, DX), BF16),
                pltpu.VMEM((rows, DX), BF16),
                pltpu.VMEM((16, share, DX), BF16),
                pltpu.VMEM((16, share, DX), BF16),
                pltpu.VMEM((16, share, 512), BF16),
                pltpu.VMEM((rows, 512), BF16),
                pltpu.VMEM((D, 256), F32),
                pltpu.VMEM((16, W, 256), F32),
            ]
            + [sem] * 14,
            compiler_params=pltpu.CompilerParams(
                collective_id=0, has_side_effects=True, vmem_limit_bytes=60 * 2**20
            ),
        )(enc_i, enc_t, w_i, w_t, dw_i, dw_t, scalars)

    in_specs = (
        P("dp", None),
        P("dp", None),
        P(None, "tensor"),
        P(None, "tensor"),
        P(None, "tensor"),
        P(None, "tensor"),
        P(),
        P(),
    )
    out_specs = (P("dp", "tensor"), P("dp", "tensor"))
    return jax.shard_map(local, mesh=mesh, in_specs=in_specs, out_specs=out_specs, check_vma=False)
```

time: 1090 us -> 178 us (0.16)
  the two profiles are of different devices: /device:TPU:1 before, /device:TPU:14 now
where the time goes in v1:
time: 178 us
  Pallas kernels  166 us (93%)
  local copies, waits for them, and re-layouts  9.98 us (6%)
  between operations  1.93 us (1%)
    pallas_call x1, Pallas kernels, local(): pl.pallas_call(functools.partial(kernel, nz, nx, D, W), out_shape=[jax.Sh...  166 us
    unnamed x6, local copies, waits for them, and re-layouts  9.98 us

profile of v1, /device:TPU:14, one launch (start us, length us, event | category | flops | bytes accessed | tf_op | source)
XLA Modules:
  0.0 178.1 jit_solution(15692292862702887776)
XLA Ops:
  1.9 0.6 pad_maximum_fusion.scalars
  2.5 1.8 %copy.10.w_i = bf16[1152,72]{1,0:T(8,128)(2,1)} copy(bf16[1152,72]{0,1:T(8,128)(2,1)} %param.10) | data formatting | bytes 331776 | tf_op args[2]
  4.3 1.8 %copy.11.w_t = bf16[1152,72]{1,0:T(8,128)(2,1)} copy(bf16[1152,72]{0,1:T(8,128)(2,1)} %param.11) | data formatting | bytes 331776 | tf_op args[3]
  6.1 1.8 %copy.12.dw_i = bf16[1152,72]{1,0:T(8,128)(2,1)} copy(bf16[1152,72]{0,1:T(8,128)(2,1)} %param.12) | data formatting | bytes 331776 | tf_op args[4]
  7.9 1.8 %copy.13.dw_t = bf16[1152,72]{1,0:T(8,128)(2,1)} copy(bf16[1152,72]{0,1:T(8,128)(2,1)} %param.13) | data formatting | bytes 331776 | tf_op args[5]
  9.7 165.6 %shard_map.95 = (f32[72,72]{1,0:T(8,128)}, f32[72,72]{1,0:T(8,128)}) custom-call(bf16[768,1152]{1,0:T(8,128)(2,1)} %enc_i.1, bf16[768,1152]{1,0:T(8,128)(2,1)} %enc_t.1, bf16[1152,72]{1,0:T(8,128)(2,1)} %copy.10.w_i, bf16[1152,72]{1,0:T(8,128)(2,1)} %copy.11.w_t, bf16[1152,72]{1,0:T(8,128)(2,1)} %copy.12.dw_i, bf16[1152,72]{1,0:T(8,128)(2,1)} %copy.13.dw_t, ...), custom_call_target="tpu_custom_call" | custom-call | tf_op jit(solution)/shard_map/pallas_call | solution.py:398
  175.3 1.4 copy.18
  176.7 1.4 copy.19

commit v2 on v1

v2 whole, which is shorter than its diff:
```python
import functools

import jax
import jax.numpy as jnp
from jax import lax
from jax.experimental import pallas as pl
from jax.experimental.pallas import tpu as pltpu
from jax.sharding import PartitionSpec as P

EPS = 1e-06
MESH = pl.DeviceIdType.MESH
F32 = jnp.float32
BF16 = jnp.bfloat16

Z_SLOTS = (0, 1, -1, 2, -2, 3, -3, 4)
XY_SLOTS = tuple(
    sorted(((i, j) for i in (0, 1, -1, 2) for j in (0, 1, -1, 2)), key=lambda p: abs(p[0]) + abs(p[1]))
)


def mirrored(back, period):
    return back if 2 * abs(back) == period else -back


def dot_nn(a, b):
    return lax.dot_general(a, b, (((1,), (0,)), ((), ())), preferred_element_type=F32)


def dot_nt(a, b):
    return lax.dot_general(a, b, (((1,), (1,)), ((), ())), preferred_element_type=F32)


def dot_tn(a, b):
    return lax.dot_general(a, b, (((0,), (0,)), ((), ())), preferred_element_type=F32)


def split_hi(value):
    hi = value.astype(BF16)
    lo = (value - hi.astype(F32)).astype(BF16)
    return hi, lo


def lanes_of(values, rows):
    lane = lax.broadcasted_iota(jnp.int32, (rows, 128), 1)
    out = jnp.zeros((rows, 128), F32)
    for index, value in enumerate(values):
        out = jnp.where(lane == index, value.astype(F32), out)
    return out


def kernel(
    nz, nx, D, W,
    enc_i, enc_t, w_i, w_t, dw_i, dw_t, scalars,
    out_i, out_t,
    wpad, x_buf, x_got, raw, img, txt, gi, pb_buf, at_buf, csum,
    si_buf, st_buf, sib_got, ri_buf, rt_buf, stage, cols, hv, hv_got, ent_i, ent_t,
    fs, fr, ais, air, ats, atr, gs, gr, ris, rir, rts, rtr, bs, br, hs, hr,
):
    dp = lax.axis_index("dp")
    tp = lax.axis_index("tensor")
    z, h = dp // 2, dp % 2
    y, x, c = h * 2 + tp // (2 * nx), (tp // 2) % nx, tp % 2
    rows = enc_i.shape[0]
    share = rows // 16
    half = 16 * share
    DX = D + 128
    DE = 2 * D + 128
    s = scalars[0]
    bias = scalars[1]

    def device_at(dz, dy, dx, core):
        zz, yy, xx = (z - dz + nz) % nz, (y - dy + 4) % 4, (x - dx + nx) % nx
        return (zz * 2 + yy // 2, ((yy % 2) * nx + xx) * 2 + core)

    tp_ids = [(tp + q) % 16 for q in range(16)]
    z_ids = [device_at(b, 0, 0, c) for b in Z_SLOTS]
    xy_ids = [device_at(0, dy, dx, c) for dx, dy in XY_SLOTS]
    z_back = [Z_SLOTS.index(mirrored(b, nz)) for b in Z_SLOTS]
    xy_back = [XY_SLOTS.index((mirrored(dx, nx), mirrored(dy, 4))) for dx, dy in XY_SLOTS]

    started = []

    def send(src, dst, ssem, rsem, device):
        copy = pltpu.make_async_remote_copy(
            src_ref=src, dst_ref=dst, send_sem=ssem, recv_sem=rsem,
            device_id=device, device_id_type=MESH,
        )
        copy.start()
        started.append(copy)

    def arrived(dst, rsem):
        pltpu.make_async_remote_copy(
            src_ref=dst, dst_ref=dst, send_sem=fs.at[0], recv_sem=rsem,
            device_id=(dp, tp), device_id_type=MESH,
        ).wait_recv()

    barrier = pltpu.get_barrier_semaphore()
    peers = [(dp, tp_ids[q]) for q in range(1, 16)]
    peers += [(z * 2 + 1 - h, (tp + 2 * q) % 16) for q in range(8)]
    peers += [((dp + q) % 16, tp) for q in range(2, 15)]
    peers += [((dp + 15 - 14 * h) % 16, tp)]
    for peer in peers:
        pl.semaphore_signal(barrier, inc=1, device_id=peer, device_id_type=MESH)

    wpad[...] = jnp.zeros_like(wpad)
    wpad[0:W] = w_i[...]
    wpad[128 : 128 + W] = dw_i[...]
    wpad[256 : 256 + W] = w_t[...]
    wpad[384 : 384 + W] = dw_t[...]

    def project(r, carry):
        at = pl.ds(pl.multiple_of(r * 256, 256), 256)
        x_buf[at, 0:256] = dot_nt(enc_i[at, :], wpad[0:256]).astype(BF16)
        x_buf[at, 256:512] = dot_nt(enc_t[at, :], wpad[256:512]).astype(BF16)
        return carry

    lax.fori_loop(0, rows // 256, project, 0)
    pl.semaphore_wait(barrier, len(peers))

    def share_at(index):
        return pl.ds(pl.multiple_of(index * share, share), share)

    for q in range(1, 16):
        send(x_buf.at[share_at(tp_ids[q]), :], x_got.at[tp], fs.at[q], fr.at[tp], (dp, tp_ids[q]))
    x_got[pl.ds(tp, 1)] = x_buf[share_at(tp), :].reshape(1, share, 512)
    for q in range(1, 16):
        arrived(x_got.at[tp_ids[q]], fr.at[tp_ids[q]])
    for q in range(16):
        for k in range(4):
            raw[k, :, q * W : (q + 1) * W] = x_got[q, :, k * 128 : k * 128 + W].astype(F32)

    def unit_parts(values, tangent):
        radius = jnp.sqrt(jnp.sum(values * values, axis=1, keepdims=True) + EPS)
        unit = values / radius
        rate = jnp.sum(unit * tangent, axis=1, keepdims=True)
        unit_tangent = (tangent - unit * rate) / radius
        return unit, unit_tangent, radius, rate / radius

    for k, buf in ((0, img), (2, txt)):
        unit, tangent, radius, ratio = unit_parts(raw[k], raw[k + 1])
        buf[0:share, 0:D] = unit.astype(BF16)
        buf[0:share, D : 2 * D] = tangent.astype(BF16)
        hi, lo = split_hi(ratio)
        buf[0:share, 2 * D : DE] = lanes_of((hi, lo), share).astype(BF16)

    parts = ((0, D), (D, DE - D))
    counts = {"i": 0, "t": 0}
    sib = (dp, tp + 1 - 2 * c)

    def ipart(slot, part):
        return img.at[pl.ds(slot * share, share), pl.ds(*parts[part])]

    def tat(slot):
        return txt.at[pl.ds(slot * share, share), :]

    def isend(src, dst, part, device):
        send(ipart(src, part), ipart(dst, part), ais.at[counts["i"]], air.at[part * 32 + dst], device)
        counts["i"] += 1

    def hop(pos, axis, way, part):
        to = list(pos)
        to[axis] = 2 if abs(pos[axis] + way) == 2 else pos[axis] + way
        away = [0, 0]
        away[axis] = -way
        isend(XY_SLOTS.index(pos), XY_SLOTS.index(tuple(to)), part, device_at(0, away[1], away[0], c))

    def i_on(pos, part):
        first, second = (0, 1) if part == 0 else (1, 0)
        if pos[second] == 0:
            if pos[first] >= 0 and (pos[first] == 0 or (part == 0 and pos[first] == 1)):
                hop(pos, first, 1, part)
            if pos[first] == 0 or (part == 1 and pos[first] == -1):
                hop(pos, first, -1, part)
            hop(pos, second, 1, part)
            hop(pos, second, -1, part)
        else:
            forth = pos[first] in (0, 2)
            if pos[second] == 1 and forth:
                hop(pos, second, 1, part)
            if pos[second] == -1 and not forth:
                hop(pos, second, -1, part)
        isend(XY_SLOTS.index(pos), 16 + XY_SLOTS.index(pos), part, sib)

    def i_step(pos):
        for part in (0, 1):
            slot = XY_SLOTS.index(pos)
            arrived(ipart(slot, part), air.at[part * 32 + slot])
            i_on(pos, part)

    def tsend(src, dst, device):
        send(tat(src), tat(dst), ats.at[counts["t"]], atr.at[dst], device)
        counts["t"] += 1

    def t_on(back):
        src = Z_SLOTS.index(back)
        if 0 <= back < 3:
            tsend(src, Z_SLOTS.index(back + 1), device_at(-1, 0, 0, c))
        if -3 < back <= 0:
            tsend(src, Z_SLOTS.index(back - 1), device_at(1, 0, 0, c))

    def twait(back):
        slot = Z_SLOTS.index(back)
        arrived(tat(slot), atr.at[slot])

    for part in (0, 1):
        i_on((0, 0), part)
    t_on(0)
    for k in range(D // 128):
        ka = pl.ds(k * 128, 128)
        ent_i[ka, :] = enc_i[:, ka].T
        ent_t[ka, :] = enc_t[:, ka].T
    for pos in XY_SLOTS[1:5]:
        i_step(pos)
    for back in (1, -1):
        twait(back)
        t_on(back)
    for pos in XY_SLOTS[5:11]:
        i_step(pos)
    for back in (2, -2):
        twait(back)
        t_on(back)
    for pos in XY_SLOTS[11:16]:
        i_step(pos)
    for back in (3, -3):
        twait(back)
    far = Z_SLOTS.index(3) + c * (Z_SLOTS.index(-3) - Z_SLOTS.index(3))
    tsend(pl.multiple_of(far, 1), Z_SLOTS.index(4), device_at(2 * c - 1, 0, 0, c))
    for slot in range(16):
        for part in (0, 1):
            arrived(ipart(16 + slot, part), air.at[part * 32 + 16 + slot])

    eye = lanes_of([(lax.broadcasted_iota(jnp.int32, (8, 1), 0) == k) for k in range(8)], 8).astype(BF16)
    TC = 4 * share
    RB = 4 * share

    def chunk(ci, between):
        at = pl.ds(ci * TC, TC)
        ends = txt[at, 2 * D : DE].astype(F32)
        sigma = ends[:, 0:1] + ends[:, 1:2]
        csum[...] = jnp.zeros_like(csum)

        def block(r, carry):
            ra = pl.ds(pl.multiple_of(r * RB, RB), RB)
            tu = txt[at, 0:D]
            tt = txt[at, D : 2 * D]
            iu = img[ra, 0:D]
            it = img[ra, D : 2 * D]
            extra = img[ra, 2 * D : DE].astype(F32)
            rho = extra[:, 0:1] + extra[:, 1:2]
            cosine = dot_nt(iu, tu)
            cross = dot_nt(it, tu) + dot_nt(iu, tt)
            prob = jax.nn.sigmoid(s * cosine + bias)
            rate = prob * (1.0 - prob) * (s * cross)
            pb = prob.astype(BF16)
            q1 = prob * cosine
            q2 = prob * cross + rate * cosine
            csum[0:1, :] += jnp.sum(q1, axis=0, keepdims=True)
            csum[1:2, :] += jnp.sum(q2, axis=0, keepdims=True)
            rb = rate.astype(BF16)
            pb_buf[ra, :] = pb
            at_buf[ra, :] = rb
            gain = dot_nn(rb, tu) + dot_nn(pb, tt) - rho * dot_nn(pb, tu)
            sums = lanes_of((jnp.sum(q1, axis=1, keepdims=True), jnp.sum(q2, axis=1, keepdims=True)), RB)
            if ci == 0:
                gi[ra, 0:D] = gain
                gi[ra, D:DX] = sums
            else:
                gi[ra, 0:D] += gain
                gi[ra, D:DX] += sums
            return carry

        lax.fori_loop(half // RB, 2 * half // RB, block, 0)
        between()
        lax.fori_loop(0, half // RB, block, 0)

        hi, lo = split_hi(csum[...])
        tops = jnp.concatenate([hi[0:2].astype(F32), lo[0:2].astype(F32), jnp.zeros((4, TC), F32)], axis=0)
        st_buf[at, D:DX] = dot_tn(tops.astype(BF16), eye).astype(BF16)

        def columns(k, carry):
            ka = pl.ds(pl.multiple_of(k * 384, 128), 384)
            kb = pl.ds(pl.multiple_of(D + k * 384, 128), 384)
            gain = dot_tn(at_buf[...], img[:, ka]) + dot_tn(pb_buf[...], img[:, kb])
            st_buf[at, ka] = (gain - sigma * dot_tn(pb_buf[...], img[:, ka])).astype(BF16)
            return carry

        lax.fori_loop(0, D // 384, columns, 0)
        for q in range(4 * ci, 4 * ci + 4):
            if q > 0:
                k = z_back[q]
                send(st_buf.at[pl.ds(q * share, share), :], rt_buf.at[k], rts.at[q], rtr.at[k], z_ids[q])

    def sums_out(row, extra):
        at = pl.ds(row, share)
        total, ends = gi[at, 0:D], gi[at, D:DX]
        inner, inner_rate = ends[:, 0:1], ends[:, 1:2]
        if extra is not None:
            total = total + extra[:, 0:D].astype(F32)
            ends = extra[:, D:DX].astype(F32)
            inner = inner + (ends[:, 0:1] + ends[:, 2:3])
            inner_rate = inner_rate + (ends[:, 1:2] + ends[:, 3:4])
        si_buf[at, 0:D] = total.astype(BF16)
        (ih, il), (rh, rl) = split_hi(inner), split_hi(inner_rate)
        si_buf[at, D:DX] = lanes_of((ih, rh, il, rl), share).astype(BF16)

    def nothing():
        pass

    def to_sibling():
        for g in range(4):
            def one(q, carry):
                sums_out(pl.multiple_of(half + (4 * g + q) * share, share), None)
                return carry
            lax.fori_loop(0, 4, one, 0)
            src = si_buf.at[pl.ds(half + 4 * g * share, 4 * share), :]
            send(src, sib_got.at[pl.ds(4 * g * share, 4 * share), :], gs.at[g], gr.at[g], sib)

    chunk(0, nothing)
    twait(4)
    chunk(1, to_sibling)

    for g in range(4):
        arrived(sib_got.at[pl.ds(4 * g * share, 4 * share), :], gr.at[g])
        for q in range(4 * g, 4 * g + 4):
            if q > 0:
                qa = pl.ds(q * share, share)
                sums_out(q * share, sib_got[qa, :])
                k = xy_back[q]
                send(si_buf.at[qa, :], ri_buf.at[k], ris.at[q], rir.at[k], xy_ids[q])

    for q in range(1, 8):
        arrived(rt_buf.at[q], rtr.at[q])
    for q in range(1, 16):
        arrived(ri_buf.at[q], rir.at[q])

    iu, it = img[0:share, 0:D].astype(F32), img[0:share, D : 2 * D].astype(F32)
    tu, tt = txt[0:share, 0:D].astype(F32), txt[0:share, D : 2 * D].astype(F32)
    pair_cos = jnp.sum(iu * tu, axis=1, keepdims=True)
    pair_cross = jnp.sum(it * tu + iu * tt, axis=1, keepdims=True)
    stage[...] = jnp.zeros_like(stage)
    for k, got in ((0, ri_buf), (1, rt_buf)):
        if k == 0:
            total = gi[0:share, 0:D]
            inner = gi[0:share, D : D + 1]
            inner_rate = gi[0:share, D + 1 : D + 2]
            more = [sib_got[0:share, :]] + [got[q] for q in range(1, 16)]
            other, other_tangent = tu, tt
        else:
            total, inner, inner_rate = 0.0, 0.0, 0.0
            more = [st_buf[0:share, :]] + [got[q] for q in range(1, 8)]
            other, other_tangent = iu, it
        for term in more:
            total = total + term[:, 0:D].astype(F32)
            ends = term[:, D:DX].astype(F32)
            inner = inner + (ends[:, 0:1] + ends[:, 2:3])
            inner_rate = inner_rate + (ends[:, 1:2] + ends[:, 3:4])
        unit, tangent, radius, ratio = unit_parts(raw[2 * k], raw[2 * k + 1])
        total = s * (total + (ratio * other - other_tangent))
        inner = s * (inner - pair_cos)
        inner_rate = s * (inner_rate - pair_cross)
        raw[2 * k] = (total - tangent * inner - unit * (inner_rate - ratio * inner)) / radius
        for q in range(16):
            hi, lo = split_hi(raw[2 * k, :, q * W : (q + 1) * W])
            stage[q, :, k * 256 : k * 256 + W] = hi
            stage[q, :, k * 256 + 128 : k * 256 + 128 + W] = lo

    for q in range(1, 16):
        send(stage.at[tp_ids[q]], cols.at[share_at(tp), :], bs.at[q], br.at[tp], (dp, tp_ids[q]))
    cols[share_at(tp), :] = stage[pl.ds(tp, 1)].reshape(share, 512)
    for q in range(1, 16):
        arrived(cols.at[share_at(tp_ids[q]), :], br.at[tp_ids[q]])

    def head(k, carry):
        ka = pl.ds(pl.multiple_of(k * 128, 128), 128)
        both = dot_nn(ent_i[ka, :], cols[:, 0:256])
        hv[ka, 0:128] = both[:, 0:128] + both[:, 128:256]
        both = dot_nn(ent_t[ka, :], cols[:, 256:512])
        hv[ka, 128:256] = both[:, 0:128] + both[:, 128:256]
        return carry

    lax.fori_loop(0, D // 128, head, 0)

    def own_rows(index):
        return pl.ds(pl.multiple_of(index * W, 8), W)

    for q in range(1, 16):
        to = (dp + q) % 16
        send(hv.at[own_rows(to), :], hv_got.at[16 - q], hs.at[q], hr.at[16 - q], (to, tp))
    total = hv[own_rows(dp), :]
    for q in range(1, 16):
        arrived(hv_got.at[q], hr.at[q])
        total = total + hv_got[q]
    out_i[...] = total[:, 0:W]
    out_t[...] = total[:, 128 : 128 + W]
    for copy in started:
        copy.wait_send()


def solution(mesh):
    nz = mesh.shape["dp"] // 2
    nx = mesh.shape["tensor"] // 4

    def local(enc_i, enc_t, w_i, w_t, dw_i, dw_t, sharpness, offset):
        rows, D = enc_i.shape
        W = w_i.shape[1]
        share = rows // 16
        DX, DE = D + 128, 2 * D + 128
        scalars = jnp.concatenate([sharpness, offset])
        vmem = pl.BlockSpec(memory_space=pltpu.VMEM)
        sem = lambda n: pltpu.SemaphoreType.DMA((n,))
        return pl.pallas_call(
            functools.partial(kernel, nz, nx, D, W),
            out_shape=[jax.ShapeDtypeStruct((W, W), F32)] * 2,
            in_specs=[vmem] * 6 + [pl.BlockSpec(memory_space=pltpu.SMEM)],
            out_specs=[vmem] * 2,
            scratch_shapes=[
                pltpu.VMEM((512, D), BF16),
                pltpu.VMEM((rows, 512), BF16),
                pltpu.VMEM((16, share, 512), BF16),
                pltpu.VMEM((4, share, D), F32),
                pltpu.VMEM((32 * share, DE), BF16),
                pltpu.VMEM((8 * share, DE), BF16),
                pltpu.VMEM((32 * share, DX), F32),
                pltpu.VMEM((32 * share, 4 * share), BF16),
                pltpu.VMEM((32 * share, 4 * share), BF16),
                pltpu.VMEM((8, 4 * share), F32),
                pltpu.VMEM((32 * share, DX), BF16),
                pltpu.VMEM((8 * share, DX), BF16),
                pltpu.VMEM((16 * share, DX), BF16),
                pltpu.VMEM((16, share, DX), BF16),
                pltpu.VMEM((8, share, DX), BF16),
                pltpu.VMEM((16, share, 512), BF16),
                pltpu.VMEM((rows, 512), BF16),
                pltpu.VMEM((D, 256), F32),
                pltpu.VMEM((16, W, 256), F32),
                pltpu.VMEM((D, rows), BF16),
                pltpu.VMEM((D, rows), BF16),
            ]
            + [sem(n) for n in (16, 16, 64, 64, 8, 8, 4, 4, 16, 16, 8, 8, 16, 16, 16, 16)],
            compiler_params=pltpu.CompilerParams(
                collective_id=0, has_side_effects=True, vmem_limit_bytes=60 * 2**20
            ),
        )(enc_i, enc_t, w_i.T, w_t.T, dw_i.T, dw_t.T, scalars)

    in_specs = (
        P("dp", None),
        P("dp", None),
        P(None, "tensor"),
        P(None, "tensor"),
        P(None, "tensor"),
        P(None, "tensor"),
        P(),
        P(),
    )
    out_specs = (P("dp", "tensor"), P("dp", "tensor"))
    return jax.shard_map(local, mesh=mesh, in_specs=in_specs, out_specs=out_specs, check_vma=False)
```

time: 178 us -> 159 us (0.89)
  the two profiles are of different devices: /device:TPU:14 before, /device:TPU:1 now
where the time goes in v2:
time: 159 us
  Pallas kernels  153 us (96%)
  local copies, waits for them, and re-layouts  2.77 us (2%)
  between operations  1.93 us (1%)
    pallas_call x1, Pallas kernels, local(): pl.pallas_call(functools.partial(kernel, nz, nx, D, W), out_shape=[jax.Sh...  153 us

profile of v2, /device:TPU:1, one launch (start us, length us, event | category | flops | bytes accessed | tf_op | source)
XLA Modules:
  0.0 158.8 jit_solution(4404947571364715047)
XLA Ops:
  1.9 0.6 pad_maximum_fusion.scalars
  2.5 153.5 %shard_map.95 = (f32[72,72]{1,0:T(8,128)}, f32[72,72]{1,0:T(8,128)}) custom-call(bf16[768,1152]{1,0:T(8,128)(2,1)} %enc_i.1, bf16[768,1152]{1,0:T(8,128)(2,1)} %enc_t.1, bf16[72,1152]{1,0:T(8,128)(2,1)} %bitcast.4, bf16[72,1152]{1,0:T(8,128)(2,1)} %bitcast.5, bf16[72,1152]{1,0:T(8,128)(2,1)} %bitcast.6, bf16[72,1152]{1,0:T(8,128)(2,1)} %bitcast.7, ...), custom_call_target="tpu_custom_call" | custom-call | tf_op jit(solution)/shard_map/pallas_call | solution.py:411
  156.0 1.4 copy.14
  157.4 1.4 copy.15

commit v3 on v2

--- a/solution.py
+++ b/solution.py
@@ -53,7 +53,7 @@
     enc_i, enc_t, w_i, w_t, dw_i, dw_t, scalars,
     out_i, out_t,
     wpad, x_buf, x_got, raw, img, txt, gi, pb_buf, at_buf, csum,
-    si_buf, st_buf, sib_got, ri_buf, rt_buf, stage, cols, hv, hv_got, ent_i, ent_t,
+    si_buf, st_buf, sib_got, ri_buf, rt_buf, stage, tmp, cols, hv, hp, hv_got, ent_i, ent_t,
     fs, fr, ais, air, ats, atr, gs, gr, ris, rir, rts, rtr, bs, br, hs, hr,
 ):
     dp = lax.axis_index("dp")
@@ -65,6 +65,9 @@
     half = 16 * share
     DX = D + 128
     DE = 2 * D + 128
+    T0 = 80
+    T1 = 128 - T0
+    T2 = W - T1
     s = scalars[0]
     bias = scalars[1]
 
@@ -105,13 +108,16 @@
     wpad[...] = jnp.zeros_like(wpad)
     wpad[0:W] = w_i[...]
     wpad[128 : 128 + W] = dw_i[...]
-    wpad[256 : 256 + W] = w_t[...]
-    wpad[384 : 384 + W] = dw_t[...]
+    wpad[256 + T0 : 384] = w_t[0:T1]
+    wpad[384 + T0 : 512] = dw_t[0:T1]
+    wpad[512 : 512 + T2] = w_t[T1:W]
+    wpad[544 : 544 + T2] = dw_t[T1:W]
 
     def project(r, carry):
         at = pl.ds(pl.multiple_of(r * 256, 256), 256)
-        x_buf[at, 0:256] = dot_nt(enc_i[at, :], wpad[0:256]).astype(BF16)
-        x_buf[at, 256:512] = dot_nt(enc_t[at, :], wpad[256:512]).astype(BF16)
+        text = enc_t[at, :]
+        x_buf[at, 0:256] = (dot_nt(enc_i[at, :], wpad[0:256]) + dot_nt(text, wpad[256:512])).astype(BF16)
+        x_buf[at, 256:384] = dot_nt(text, wpad[512:640]).astype(BF16)
         return carry
 
     lax.fori_loop(0, rows // 256, project, 0)
@@ -122,12 +128,17 @@
 
     for q in range(1, 16):
         send(x_buf.at[share_at(tp_ids[q]), :], x_got.at[tp], fs.at[q], fr.at[tp], (dp, tp_ids[q]))
-    x_got[pl.ds(tp, 1)] = x_buf[share_at(tp), :].reshape(1, share, 512)
+    x_got[pl.ds(tp, 1)] = x_buf[share_at(tp), :].reshape(1, share, 384)
     for q in range(1, 16):
         arrived(x_got.at[tp_ids[q]], fr.at[tp_ids[q]])
     for q in range(16):
-        for k in range(4):
-            raw[k, :, q * W : (q + 1) * W] = x_got[q, :, k * 128 : k * 128 + W].astype(F32)
+        last = x_got[q, :, 256:384].astype(F32)
+        for k in range(2):
+            tile = x_got[q, :, k * 128 : k * 128 + 128].astype(F32)
+            raw[k, :, q * W : (q + 1) * W] = tile[:, 0:W]
+            raw[2 + k, :, q * W : q * W + T1] = pltpu.roll(tile, T1, 1)[:, 0:T1]
+            rest = last if k == 0 else pltpu.roll(last, 96, 1)
+            raw[2 + k, :, q * W + T1 : (q + 1) * W] = rest[:, 0:T2]
 
     def unit_parts(values, tangent):
         radius = jnp.sqrt(jnp.sum(values * values, axis=1, keepdims=True) + EPS)
@@ -209,35 +220,17 @@
         ka = pl.ds(k * 128, 128)
         ent_i[ka, :] = enc_i[:, ka].T
         ent_t[ka, :] = enc_t[:, ka].T
-    for pos in XY_SLOTS[1:5]:
-        i_step(pos)
-    for back in (1, -1):
-        twait(back)
-        t_on(back)
-    for pos in XY_SLOTS[5:11]:
-        i_step(pos)
-    for back in (2, -2):
-        twait(back)
-        t_on(back)
-    for pos in XY_SLOTS[11:16]:
-        i_step(pos)
-    for back in (3, -3):
-        twait(back)
-    far = Z_SLOTS.index(3) + c * (Z_SLOTS.index(-3) - Z_SLOTS.index(3))
-    tsend(pl.multiple_of(far, 1), Z_SLOTS.index(4), device_at(2 * c - 1, 0, 0, c))
-    for slot in range(16):
-        for part in (0, 1):
-            arrived(ipart(16 + slot, part), air.at[part * 32 + 16 + slot])
-
     eye = lanes_of([(lax.broadcasted_iota(jnp.int32, (8, 1), 0) == k) for k in range(8)], 8).astype(BF16)
+    first_two = jnp.where(lax.broadcasted_iota(jnp.int32, (8, 128), 1) < 2, 1.0, 0.0).astype(BF16)
     TC = 4 * share
-    RB = 4 * share
-
-    def chunk(ci, between):
+    RB = 8 * share
+
+    def prepare(ci):
+        csum[...] = jnp.zeros_like(csum)
+        return dot_nt(first_two, txt[ci * TC : (ci + 1) * TC, 2 * D : DE])[0:1, :]
+
+    def blocks(ci, sigma, low, high):
         at = pl.ds(ci * TC, TC)
-        ends = txt[at, 2 * D : DE].astype(F32)
-        sigma = ends[:, 0:1] + ends[:, 1:2]
-        csum[...] = jnp.zeros_like(csum)
 
         def block(r, carry):
             ra = pl.ds(pl.multiple_of(r * RB, RB), RB)
@@ -256,10 +249,9 @@
             q2 = prob * cross + rate * cosine
             csum[0:1, :] += jnp.sum(q1, axis=0, keepdims=True)
             csum[1:2, :] += jnp.sum(q2, axis=0, keepdims=True)
-            rb = rate.astype(BF16)
             pb_buf[ra, :] = pb
-            at_buf[ra, :] = rb
-            gain = dot_nn(rb, tu) + dot_nn(pb, tt) - rho * dot_nn(pb, tu)
+            at_buf[ra, :] = (rate - sigma * prob).astype(BF16)
+            gain = dot_nn((rate - rho * prob).astype(BF16), tu) + dot_nn(pb, tt)
             sums = lanes_of((jnp.sum(q1, axis=1, keepdims=True), jnp.sum(q2, axis=1, keepdims=True)), RB)
             if ci == 0:
                 gi[ra, 0:D] = gain
@@ -269,22 +261,17 @@
                 gi[ra, D:DX] += sums
             return carry
 
-        lax.fori_loop(half // RB, 2 * half // RB, block, 0)
-        between()
-        lax.fori_loop(0, half // RB, block, 0)
-
+        lax.fori_loop(low, high, block, 0)
+
+    def text_sums(ci):
+        at = pl.ds(ci * TC, TC)
         hi, lo = split_hi(csum[...])
         tops = jnp.concatenate([hi[0:2].astype(F32), lo[0:2].astype(F32), jnp.zeros((4, TC), F32)], axis=0)
         st_buf[at, D:DX] = dot_tn(tops.astype(BF16), eye).astype(BF16)
-
-        def columns(k, carry):
-            ka = pl.ds(pl.multiple_of(k * 384, 128), 384)
-            kb = pl.ds(pl.multiple_of(D + k * 384, 128), 384)
-            gain = dot_tn(at_buf[...], img[:, ka]) + dot_tn(pb_buf[...], img[:, kb])
-            st_buf[at, ka] = (gain - sigma * dot_tn(pb_buf[...], img[:, ka])).astype(BF16)
-            return carry
-
-        lax.fori_loop(0, D // 384, columns, 0)
+        for k in range(0, D, 256):
+            e = min(k + 256, D)
+            gain = dot_tn(at_buf[...], img[:, k:e]) + dot_tn(pb_buf[...], img[:, D + k : D + e])
+            st_buf[at, k:e] = gain.astype(BF16)
         for q in range(4 * ci, 4 * ci + 4):
             if q > 0:
                 k = z_back[q]
@@ -303,9 +290,6 @@
         (ih, il), (rh, rl) = split_hi(inner), split_hi(inner_rate)
         si_buf[at, D:DX] = lanes_of((ih, rh, il, rl), share).astype(BF16)
 
-    def nothing():
-        pass
-
     def to_sibling():
         for g in range(4):
             def one(q, carry):
@@ -315,9 +299,38 @@
             src = si_buf.at[pl.ds(half + 4 * g * share, 4 * share), :]
             send(src, sib_got.at[pl.ds(4 * g * share, 4 * share), :], gs.at[g], gr.at[g], sib)
 
-    chunk(0, nothing)
+    for pos in XY_SLOTS[1:5]:
+        i_step(pos)
+    for back in (1, -1):
+        twait(back)
+        t_on(back)
+    for pos in XY_SLOTS[5:8]:
+        i_step(pos)
+    twait(2)
+    t_on(2)
+    sigma = prepare(0)
+    blocks(0, sigma, 0, 1)
+    for pos in XY_SLOTS[8:11]:
+        i_step(pos)
+    twait(-2)
+    t_on(-2)
+    for pos in XY_SLOTS[11:16]:
+        i_step(pos)
+    blocks(0, sigma, 1, 2)
+    for back in (3, -3):
+        twait(back)
+    far = Z_SLOTS.index(3) + c * (Z_SLOTS.index(-3) - Z_SLOTS.index(3))
+    tsend(far, Z_SLOTS.index(4), device_at(2 * c - 1, 0, 0, c))
+    for slot in range(16):
+        for part in (0, 1):
+            arrived(ipart(16 + slot, part), air.at[part * 32 + 16 + slot])
+    blocks(0, sigma, 2, 4)
+    text_sums(0)
     twait(4)
-    chunk(1, to_sibling)
+    sigma = prepare(1)
+    blocks(1, sigma, 2, 4)
+    to_sibling()
+    blocks(1, sigma, 0, 2)
 
     for g in range(4):
         arrived(sib_got.at[pl.ds(4 * g * share, 4 * share), :], gr.at[g])
@@ -327,6 +340,7 @@
                 sums_out(q * share, sib_got[qa, :])
                 k = xy_back[q]
                 send(si_buf.at[qa, :], ri_buf.at[k], ris.at[q], rir.at[k], xy_ids[q])
+    text_sums(1)
 
     for q in range(1, 8):
         arrived(rt_buf.at[q], rtr.at[q])
@@ -337,7 +351,7 @@
     tu, tt = txt[0:share, 0:D].astype(F32), txt[0:share, D : 2 * D].astype(F32)
     pair_cos = jnp.sum(iu * tu, axis=1, keepdims=True)
     pair_cross = jnp.sum(it * tu + iu * tt, axis=1, keepdims=True)
-    stage[...] = jnp.zeros_like(stage)
+    tmp[...] = jnp.zeros_like(tmp)
     for k, got in ((0, ri_buf), (1, rt_buf)):
         if k == 0:
             total = gi[0:share, 0:D]
@@ -358,40 +372,67 @@
         total = s * (total + (ratio * other - other_tangent))
         inner = s * (inner - pair_cos)
         inner_rate = s * (inner_rate - pair_cross)
-        raw[2 * k] = (total - tangent * inner - unit * (inner_rate - ratio * inner)) / radius
-        for q in range(16):
-            hi, lo = split_hi(raw[2 * k, :, q * W : (q + 1) * W])
-            stage[q, :, k * 256 : k * 256 + W] = hi
-            stage[q, :, k * 256 + 128 : k * 256 + 128 + W] = lo
+        back = (total - tangent * inner - unit * (inner_rate - ratio * inner)) / radius
+        hi, lo = split_hi(back)
+        raw[2 * k] = hi.astype(F32)
+        raw[2 * k + 1] = lo.astype(F32)
+    for q in range(16):
+        for k in range(2):
+            tmp[:, k * 128 : k * 128 + W] = raw[k, :, q * W : (q + 1) * W]
+            tmp[:, k * 128 + T0 : k * 128 + 128] = raw[2 + k, :, q * W : q * W + T1]
+            tmp[:, 256 + 32 * k : 256 + 32 * k + T2] = raw[2 + k, :, q * W + T1 : (q + 1) * W]
+        stage[q] = tmp[...].astype(BF16)
 
     for q in range(1, 16):
         send(stage.at[tp_ids[q]], cols.at[share_at(tp), :], bs.at[q], br.at[tp], (dp, tp_ids[q]))
-    cols[share_at(tp), :] = stage[pl.ds(tp, 1)].reshape(share, 512)
+    cols[share_at(tp), :] = stage[pl.ds(tp, 1)].reshape(share, 384)
     for q in range(1, 16):
         arrived(cols.at[share_at(tp_ids[q]), :], br.at[tp_ids[q]])
+
+    lane = lax.broadcasted_iota(jnp.int32, (8, 128), 1)
+    text_lane = lax.broadcasted_iota(jnp.int32, (128, 128), 1) >= T0
 
     def head(k, carry):
         ka = pl.ds(pl.multiple_of(k * 128, 128), 128)
-        both = dot_nn(ent_i[ka, :], cols[:, 0:256])
-        hv[ka, 0:128] = both[:, 0:128] + both[:, 128:256]
-        both = dot_nn(ent_t[ka, :], cols[:, 256:512])
-        hv[ka, 128:256] = both[:, 0:128] + both[:, 128:256]
+        of_i = dot_nn(ent_i[ka, :], cols[:, 0:256])
+        of_t = dot_nn(ent_t[ka, :], cols[...])
+        hv[ka, 0:128] = jnp.where(text_lane, of_t[:, 0:128] + of_t[:, 128:256], of_i[:, 0:128] + of_i[:, 128:256])
+        rest = of_t[:, 256:384]
+        hv[ka, 128:256] = rest + pltpu.roll(rest, 96, 1)
         return carry
 
     lax.fori_loop(0, D // 128, head, 0)
 
-    def own_rows(index):
-        return pl.ds(pl.multiple_of(index * W, 8), W)
-
+    per = 128 // T2
+    places = [(W + 8 * (j // per), T2 * (j % per)) for j in range(W // 8)]
+
+    def pack(d, carry):
+        hp[d, 0:W, :] = hv[pl.ds(pl.multiple_of(d * W, 8), W), 0:128]
+        packed = {}
+        for j, (row, start) in enumerate(places):
+            part = hv[pl.ds(pl.multiple_of(d * W + 8 * j, 8), 8), 128:256]
+            if start:
+                part = pltpu.roll(part, start, 1)
+            packed[row] = jnp.where((lane >= start) & (lane < start + T2), part, packed.get(row, jnp.zeros((8, 128), F32)))
+        for row, value in packed.items():
+            hp[d, row : row + 8, :] = value
+        return carry
+
+    lax.fori_loop(0, 16, pack, 0)
     for q in range(1, 16):
         to = (dp + q) % 16
-        send(hv.at[own_rows(to), :], hv_got.at[16 - q], hs.at[q], hr.at[16 - q], (to, tp))
-    total = hv[own_rows(dp), :]
+        send(hp.at[to], hv_got.at[16 - q], hs.at[q], hr.at[16 - q], (to, tp))
+    total = hp[dp]
     for q in range(1, 16):
         arrived(hv_got.at[q], hr.at[q])
         total = total + hv_got[q]
-    out_i[...] = total[:, 0:W]
-    out_t[...] = total[:, 128 : 128 + W]
+    out_i[...] = total[0:W, 0:W]
+    out_t[:, 0:T1] = pltpu.roll(total[0:W], T1, 1)[:, 0:T1]
+    for j, (row, start) in enumerate(places):
+        part = total[row : row + 8]
+        if start:
+            part = pltpu.roll(part, 128 - start, 1)
+        out_t[8 * j : 8 * j + 8, T1:W] = part[:, 0:T2]
     for copy in started:
         copy.wait_send()
 
@@ -414,9 +455,9 @@
             in_specs=[vmem] * 6 + [pl.BlockSpec(memory_space=pltpu.SMEM)],
             out_specs=[vmem] * 2,
             scratch_shapes=[
-                pltpu.VMEM((512, D), BF16),
-                pltpu.VMEM((rows, 512), BF16),
-                pltpu.VMEM((16, share, 512), BF16),
+                pltpu.VMEM((640, D), BF16),
+                pltpu.VMEM((rows, 384), BF16),
+                pltpu.VMEM((16, share, 384), BF16),
                 pltpu.VMEM((4, share, D), F32),
                 pltpu.VMEM((32 * share, DE), BF16),
                 pltpu.VMEM((8 * share, DE), BF16),
@@ -429,10 +470,12 @@
                 pltpu.VMEM((16 * share, DX), BF16),
                 pltpu.VMEM((16, share, DX), BF16),
                 pltpu.VMEM((8, share, DX), BF16),
-                pltpu.VMEM((16, share, 512), BF16),
-                pltpu.VMEM((rows, 512), BF16),
+                pltpu.VMEM((16, share, 384), BF16),
+                pltpu.VMEM((share, 384), F32),
+                pltpu.VMEM((rows, 384), BF16),
                 pltpu.VMEM((D, 256), F32),
-                pltpu.VMEM((16, W, 256), F32),
+                pltpu.VMEM((16, W + 16, 128), F32),
+                pltpu.VMEM((16, W + 16, 128), F32),
                 pltpu.VMEM((D, rows), BF16),
                 pltpu.VMEM((D, rows), BF16),
             ]

time: 159 us -> 137 us (0.86)
  Pallas kernels: 153 us -> 131 us
    pallas_call x1, Pallas kernels: 153 us -> 131 us  [local(): pl.pallas_call(functools.partial(kernel, nz, nx, D, W), out_shape=[jax.Sh...]
where the time goes in v3:
time: 137 us; the launch traced here: 136 us
  Pallas kernels  131 us (96%)
  local copies, waits for them, and re-layouts  2.77 us (2%)
  between operations  1.93 us (1%)
    pallas_call x1, Pallas kernels, local(): pl.pallas_call(functools.partial(kernel, nz, nx, D, W), out_shape=[jax.Sh...  131 us
    unnamed x2, local copies, waits for them, and re-layouts  2.77 us

profile of v3, /device:TPU:1, one launch (start us, length us, event | category | flops | bytes accessed | tf_op | source)
XLA Modules:
  0.0 136.1 jit_solution(3653624896547218705)
XLA Ops:
  1.9 0.6 pad_maximum_fusion.scalars
  2.5 130.8 %shard_map.95 = (f32[72,72]{1,0:T(8,128)}, f32[72,72]{1,0:T(8,128)}) custom-call(bf16[768,1152]{1,0:T(8,128)(2,1)} %enc_i.1, bf16[768,1152]{1,0:T(8,128)(2,1)} %enc_t.1, bf16[72,1152]{1,0:T(8,128)(2,1)} %bitcast.4, bf16[72,1152]{1,0:T(8,128)(2,1)} %bitcast.5, bf16[72,1152]{1,0:T(8,128)(2,1)} %bitcast.6, bf16[72,1152]{1,0:T(8,128)(2,1)} %bitcast.7, ...), custom_call_target="tpu_custom_call" | custom-call | tf_op jit(solution)/shard_map/pallas_call | solution.py:452
  133.3 1.4 %copy.14 = f32[72,72]{1,0:T(8,128)} copy(f32[72,72]{1,0:T(8,128)} %get-tuple-element.4) | data formatting | bytes 41472
  134.7 1.4 %copy.15 = f32[72,72]{1,0:T(8,128)} copy(f32[72,72]{1,0:T(8,128)} %get-tuple-element.5) | data formatting | bytes 41472

commit v4 on v3

--- a/solution.py
+++ b/solution.py
@@ -12,7 +12,8 @@
 F32 = jnp.float32
 BF16 = jnp.bfloat16
 
-Z_SLOTS = (0, 1, -1, 2, -2, 3, -3, 4)
+Z_SLOTS = (0, 3, -3, 4, 1, -1, 2, -2)
+AWAY = (1, -1, 2)
 XY_SLOTS = tuple(
     sorted(((i, j) for i in (0, 1, -1, 2) for j in (0, 1, -1, 2)), key=lambda p: abs(p[0]) + abs(p[1]))
 )
@@ -38,6 +39,18 @@
     hi = value.astype(BF16)
     lo = (value - hi.astype(F32)).astype(BF16)
     return hi, lo
+
+
+def encoded(ends):
+    lane = lax.broadcasted_iota(jnp.int32, ends.shape, 1)
+    hi = ends.astype(BF16).astype(F32)
+    lo = pltpu.roll(ends - hi, 2, 1)
+    return jnp.where(lane < 2, hi, jnp.where(lane < 4, lo, 0.0)).astype(BF16)
+
+
+def decoded(ends):
+    ends = ends.astype(F32)
+    return ends + pltpu.roll(ends, 126, 1)
 
 
 def lanes_of(values, rows):
@@ -50,10 +63,10 @@
 
 def kernel(
     nz, nx, D, W,
-    enc_i, enc_t, w_i, w_t, dw_i, dw_t, scalars,
+    enc_i, enc_t, w_i, w_t, dw_i, dw_t, sharpness, offset,
     out_i, out_t,
     wpad, x_buf, x_got, raw, img, txt, gi, pb_buf, at_buf, csum,
-    si_buf, st_buf, sib_got, ri_buf, rt_buf, stage, tmp, cols, hv, hp, hv_got, ent_i, ent_t,
+    si_buf, st_buf, sib_got, first_got, next_buf, next_got, rt_buf, stage, tmp, cols, hv, hp, hv_got, ent_i, ent_t,
     fs, fr, ais, air, ats, atr, gs, gr, ris, rir, rts, rtr, bs, br, hs, hr,
 ):
     dp = lax.axis_index("dp")
@@ -68,8 +81,8 @@
     T0 = 80
     T1 = 128 - T0
     T2 = W - T1
-    s = scalars[0]
-    bias = scalars[1]
+    s = sharpness[0]
+    bias = offset[0]
 
     def device_at(dz, dy, dx, core):
         zz, yy, xx = (z - dz + nz) % nz, (y - dy + 4) % 4, (x - dx + nx) % nx
@@ -277,23 +290,31 @@
                 k = z_back[q]
                 send(st_buf.at[pl.ds(q * share, share), :], rt_buf.at[k], rts.at[q], rtr.at[k], z_ids[q])
 
-    def sums_out(row, extra):
+    def sums_out(row):
         at = pl.ds(row, share)
-        total, ends = gi[at, 0:D], gi[at, D:DX]
-        inner, inner_rate = ends[:, 0:1], ends[:, 1:2]
-        if extra is not None:
-            total = total + extra[:, 0:D].astype(F32)
-            ends = extra[:, D:DX].astype(F32)
-            inner = inner + (ends[:, 0:1] + ends[:, 2:3])
-            inner_rate = inner_rate + (ends[:, 1:2] + ends[:, 3:4])
-        si_buf[at, 0:D] = total.astype(BF16)
-        (ih, il), (rh, rl) = split_hi(inner), split_hi(inner_rate)
-        si_buf[at, D:DX] = lanes_of((ih, rh, il, rl), share).astype(BF16)
+        si_buf[at, 0:D] = gi[at, 0:D].astype(BF16)
+        si_buf[at, D:DX] = encoded(gi[at, D:DX])
+
+    H = DX // 2
+    halves = (pl.ds(0, H), pl.ds(H, H))
+    counts["r"] = 0
+
+    def rsend(src, dst, at, device):
+        send(src, dst, ris.at[counts["r"]], rir.at[at], device)
+        counts["r"] += 1
+
+    def add_in(row, part, got):
+        at = pl.ds(row, share)
+        if part == 0:
+            gi[at, 0:H] += got.astype(F32)
+        else:
+            gi[at, H:D] += got[:, 0 : D - H].astype(F32)
+            gi[at, D:DX] += decoded(got[:, D - H : H])
 
     def to_sibling():
         for g in range(4):
             def one(q, carry):
-                sums_out(pl.multiple_of(half + (4 * g + q) * share, share), None)
+                sums_out(pl.multiple_of(half + (4 * g + q) * share, share))
                 return carry
             lax.fori_loop(0, 4, one, 0)
             src = si_buf.at[pl.ds(half + 4 * g * share, 4 * share), :]
@@ -306,62 +327,92 @@
         t_on(back)
     for pos in XY_SLOTS[5:8]:
         i_step(pos)
-    twait(2)
-    t_on(2)
-    sigma = prepare(0)
-    blocks(0, sigma, 0, 1)
+    for back in (2, -2):
+        twait(back)
+        t_on(back)
     for pos in XY_SLOTS[8:11]:
         i_step(pos)
-    twait(-2)
-    t_on(-2)
-    for pos in XY_SLOTS[11:16]:
-        i_step(pos)
-    blocks(0, sigma, 1, 2)
     for back in (3, -3):
         twait(back)
     far = Z_SLOTS.index(3) + c * (Z_SLOTS.index(-3) - Z_SLOTS.index(3))
     tsend(far, Z_SLOTS.index(4), device_at(2 * c - 1, 0, 0, c))
+    for pos in XY_SLOTS[11:15]:
+        i_step(pos)
+    twait(4)
+    sigma = prepare(0)
+    blocks(0, sigma, 0, 1)
+    for pos in XY_SLOTS[15:16]:
+        i_step(pos)
+    blocks(0, sigma, 1, 2)
     for slot in range(16):
         for part in (0, 1):
             arrived(ipart(16 + slot, part), air.at[part * 32 + 16 + slot])
     blocks(0, sigma, 2, 4)
     text_sums(0)
-    twait(4)
     sigma = prepare(1)
     blocks(1, sigma, 2, 4)
     to_sibling()
     blocks(1, sigma, 0, 2)
 
+    near = (0,) + AWAY
     for g in range(4):
         arrived(sib_got.at[pl.ds(4 * g * share, 4 * share), :], gr.at[g])
         for q in range(4 * g, 4 * g + 4):
-            if q > 0:
-                qa = pl.ds(q * share, share)
-                sums_out(q * share, sib_got[qa, :])
-                k = xy_back[q]
-                send(si_buf.at[qa, :], ri_buf.at[k], ris.at[q], rir.at[k], xy_ids[q])
+            qa = pl.ds(q * share, share)
+            gi[qa, 0:D] += sib_got[qa, 0:D].astype(F32)
+            gi[qa, D:DX] += decoded(sib_got[qa, D:DX])
+            if q == 0:
+                continue
+            sums_out(q * share)
+            dx, dy = XY_SLOTS[q]
+            for part, off, keep in ((0, dy, dx), (1, dx, dy)):
+                if off:
+                    at = part * 12 + AWAY.index(mirrored(off, 4)) * 4 + near.index(keep)
+                    to = device_at(0, dy, 0, c) if part == 0 else device_at(0, 0, dx, c)
+                    rsend(si_buf.at[qa, halves[part]], first_got.at[at], at, to)
     text_sums(1)
+    for keep in AWAY + (0,):
+        for part in (0, 1):
+            row = XY_SLOTS.index((keep, 0) if part == 0 else (0, keep)) * share
+            for o in range(3):
+                at = part * 12 + o * 4 + near.index(keep)
+                arrived(first_got.at[at], rir.at[at])
+                add_in(row, part, first_got[at])
+            if keep == 0:
+                continue
+            at = part * 3 + AWAY.index(keep)
+            ra = pl.ds(row, share)
+            if part == 0:
+                next_buf[at] = gi[ra, 0:H].astype(BF16)
+                to = device_at(0, 0, keep, c)
+            else:
+                next_buf[at, :, 0 : D - H] = gi[ra, H:D].astype(BF16)
+                next_buf[at, :, D - H : H] = encoded(gi[ra, D:DX])
+                to = device_at(0, keep, 0, c)
+            k = part * 3 + AWAY.index(mirrored(keep, 4))
+            rsend(next_buf.at[at], next_got.at[k], 24 + k, to)
 
     for q in range(1, 8):
         arrived(rt_buf.at[q], rtr.at[q])
-    for q in range(1, 16):
-        arrived(ri_buf.at[q], rir.at[q])
+    for q in range(6):
+        arrived(next_got.at[q], rir.at[24 + q])
+        add_in(0, q // 3, next_got[q])
 
     iu, it = img[0:share, 0:D].astype(F32), img[0:share, D : 2 * D].astype(F32)
     tu, tt = txt[0:share, 0:D].astype(F32), txt[0:share, D : 2 * D].astype(F32)
     pair_cos = jnp.sum(iu * tu, axis=1, keepdims=True)
     pair_cross = jnp.sum(it * tu + iu * tt, axis=1, keepdims=True)
     tmp[...] = jnp.zeros_like(tmp)
-    for k, got in ((0, ri_buf), (1, rt_buf)):
+    for k in range(2):
         if k == 0:
             total = gi[0:share, 0:D]
             inner = gi[0:share, D : D + 1]
             inner_rate = gi[0:share, D + 1 : D + 2]
-            more = [sib_got[0:share, :]] + [got[q] for q in range(1, 16)]
+            more = []
             other, other_tangent = tu, tt
         else:
             total, inner, inner_rate = 0.0, 0.0, 0.0
-            more = [st_buf[0:share, :]] + [got[q] for q in range(1, 8)]
+            more = [st_buf[0:share, :]] + [rt_buf[q] for q in range(1, 8)]
             other, other_tangent = iu, it
         for term in more:
             total = total + term[:, 0:D].astype(F32)
@@ -446,13 +497,12 @@
         W = w_i.shape[1]
         share = rows // 16
         DX, DE = D + 128, 2 * D + 128
-        scalars = jnp.concatenate([sharpness, offset])
         vmem = pl.BlockSpec(memory_space=pltpu.VMEM)
         sem = lambda n: pltpu.SemaphoreType.DMA((n,))
         return pl.pallas_call(
             functools.partial(kernel, nz, nx, D, W),
             out_shape=[jax.ShapeDtypeStruct((W, W), F32)] * 2,
-            in_specs=[vmem] * 6 + [pl.BlockSpec(memory_space=pltpu.SMEM)],
+            in_specs=[vmem] * 6 + [pl.BlockSpec(memory_space=pltpu.SMEM)] * 2,
             out_specs=[vmem] * 2,
             scratch_shapes=[
                 pltpu.VMEM((640, D), BF16),
@@ -468,7 +518,9 @@
                 pltpu.VMEM((32 * share, DX), BF16),
                 pltpu.VMEM((8 * share, DX), BF16),
                 pltpu.VMEM((16 * share, DX), BF16),
-                pltpu.VMEM((16, share, DX), BF16),
+                pltpu.VMEM((24, share, DX // 2), BF16),
+                pltpu.VMEM((6, share, DX // 2), BF16),
+                pltpu.VMEM((6, share, DX // 2), BF16),
                 pltpu.VMEM((8, share, DX), BF16),
                 pltpu.VMEM((16, share, 384), BF16),
                 pltpu.VMEM((share, 384), F32),
@@ -479,11 +531,11 @@
                 pltpu.VMEM((D, rows), BF16),
                 pltpu.VMEM((D, rows), BF16),
             ]
-            + [sem(n) for n in (16, 16, 64, 64, 8, 8, 4, 4, 16, 16, 8, 8, 16, 16, 16, 16)],
+            + [sem(n) for n in (16, 16, 64, 64, 8, 8, 4, 4, 32, 32, 8, 8, 16, 16, 16, 16)],
             compiler_params=pltpu.CompilerParams(
                 collective_id=0, has_side_effects=True, vmem_limit_bytes=60 * 2**20
             ),
-        )(enc_i, enc_t, w_i.T, w_t.T, dw_i.T, dw_t.T, scalars)
+        )(enc_i, enc_t, w_i.T, w_t.T, dw_i.T, dw_t.T, sharpness, offset)
 
     in_specs = (
         P("dp", None),

time: 137 us -> 132 us (0.964)
  Pallas kernels: 131 us -> 127 us
    pallas_call x1, Pallas kernels: 131 us -> 127 us  [local(): pl.pallas_call(functools.partial(kernel, nz, nx, D, W), out_shape=[jax.Sh...]
where the time goes in v4:
time: 132 us; the launch traced here: 131 us
  Pallas kernels  127 us (96%)
  local copies, waits for them, and re-layouts  2.77 us (2%)
  between operations  1.93 us (1%)
    pallas_call x1, Pallas kernels, local(): pl.pallas_call(functools.partial(kernel, nz, nx, D, W), out_shape=[jax.Sh...  127 us
    unnamed x2, local copies, waits for them, and re-layouts  2.77 us

profile of v4, /device:TPU:1, one launch (start us, length us, event | category | flops | bytes accessed | tf_op | source)
XLA Modules:
  0.0 131.3 jit_solution(17394531465333169497)
XLA Ops:
  1.9 126.6 %shard_map.95 = (f32[72,72]{1,0:T(8,128)}, f32[72,72]{1,0:T(8,128)}) custom-call(bf16[768,1152]{1,0:T(8,128)(2,1)} %enc_i.1, bf16[768,1152]{1,0:T(8,128)(2,1)} %enc_t.1, bf16[72,1152]{1,0:T(8,128)(2,1)} %bitcast.4, bf16[72,1152]{1,0:T(8,128)(2,1)} %bitcast.5, bf16[72,1152]{1,0:T(8,128)(2,1)} %bitcast.6, bf16[72,1152]{1,0:T(8,128)(2,1)} %bitcast.7, ...), custom_call_target="tpu_custom_call" | custom-call | tf_op jit(solution)/shard_map/pallas_call | solution.py:502
  128.5 1.4 %copy.14 = f32[72,72]{1,0:T(8,128)} copy(f32[72,72]{1,0:T(8,128)} %get-tuple-element.4) | data formatting | bytes 41472
  129.9 1.4 %copy.15 = f32[72,72]{1,0:T(8,128)} copy(f32[72,72]{1,0:T(8,128)} %get-tuple-element.5) | data formatting | bytes 41472

commit v5 on v4

--- a/solution.py
+++ b/solution.py
@@ -63,9 +63,9 @@
 
 def kernel(
     nz, nx, D, W,
-    enc_i, enc_t, w_i, w_t, dw_i, dw_t, sharpness, offset,
+    from_i, from_t, w_i, w_t, dw_i, dw_t, sharpness, offset,
     out_i, out_t,
-    wpad, x_buf, x_got, raw, img, txt, gi, pb_buf, at_buf, csum,
+    enc_i, enc_t, cs, wpad, x_buf, x_got, raw, img, txt, gi, pb_buf, at_buf, csum,
     si_buf, st_buf, sib_got, first_got, next_buf, next_got, rt_buf, stage, tmp, cols, hv, hp, hv_got, ent_i, ent_t,
     fs, fr, ais, air, ats, atr, gs, gr, ris, rir, rts, rtr, bs, br, hs, hr,
 ):
@@ -110,6 +110,10 @@
             device_id=(dp, tp), device_id_type=MESH,
         ).wait_recv()
 
+    loads = [pltpu.make_async_copy(a, b, cs.at[k]) for k, (a, b) in enumerate(((from_i, enc_i), (from_t, enc_t)))]
+    for load in loads:
+        load.start()
+
     barrier = pltpu.get_barrier_semaphore()
     peers = [(dp, tp_ids[q]) for q in range(1, 16)]
     peers += [(z * 2 + 1 - h, (tp + 2 * q) % 16) for q in range(8)]
@@ -126,21 +130,28 @@
     wpad[512 : 512 + T2] = w_t[T1:W]
     wpad[544 : 544 + T2] = dw_t[T1:W]
 
-    def project(r, carry):
-        at = pl.ds(pl.multiple_of(r * 256, 256), 256)
-        text = enc_t[at, :]
-        x_buf[at, 0:256] = (dot_nt(enc_i[at, :], wpad[0:256]) + dot_nt(text, wpad[256:512])).astype(BF16)
-        x_buf[at, 256:384] = dot_nt(text, wpad[512:640]).astype(BF16)
-        return carry
-
-    lax.fori_loop(0, rows // 256, project, 0)
-    pl.semaphore_wait(barrier, len(peers))
-
     def share_at(index):
         return pl.ds(pl.multiple_of(index * share, share), share)
 
-    for q in range(1, 16):
-        send(x_buf.at[share_at(tp_ids[q]), :], x_got.at[tp], fs.at[q], fr.at[tp], (dp, tp_ids[q]))
+    for load in loads:
+        load.wait()
+
+    for step in range(2):
+        side = tp // 8 if step == 0 else 1 - tp // 8
+
+        def project(r, carry):
+            at = pl.ds(pl.multiple_of(side * (rows // 2) + r * (rows // 4), rows // 4), rows // 4)
+            text = enc_t[at, :]
+            x_buf[at, 0:256] = (dot_nt(enc_i[at, :], wpad[0:256]) + dot_nt(text, wpad[256:512])).astype(BF16)
+            x_buf[at, 256:384] = dot_nt(text, wpad[512:640]).astype(BF16)
+            return carry
+
+        lax.fori_loop(0, 2, project, 0)
+        if step == 0:
+            pl.semaphore_wait(barrier, len(peers))
+        for q in range(1 - step, 8):
+            to = side * 8 + (tp + q) % 8
+            send(x_buf.at[share_at(to), :], x_got.at[tp], fs.at[step * 8 + q], fr.at[tp], (dp, to))
     x_got[pl.ds(tp, 1)] = x_buf[share_at(tp), :].reshape(1, share, 384)
     for q in range(1, 16):
         arrived(x_got.at[tp_ids[q]], fr.at[tp_ids[q]])
@@ -155,13 +166,14 @@
 
     def unit_parts(values, tangent):
         radius = jnp.sqrt(jnp.sum(values * values, axis=1, keepdims=True) + EPS)
-        unit = values / radius
+        inverse = 1.0 / radius
+        unit = values * inverse
         rate = jnp.sum(unit * tangent, axis=1, keepdims=True)
-        unit_tangent = (tangent - unit * rate) / radius
-        return unit, unit_tangent, radius, rate / radius
+        unit_tangent = (tangent - unit * rate) * inverse
+        return unit, unit_tangent, inverse, rate * inverse
 
     for k, buf in ((0, img), (2, txt)):
-        unit, tangent, radius, ratio = unit_parts(raw[k], raw[k + 1])
+        unit, tangent, inverse, ratio = unit_parts(raw[k], raw[k + 1])
         buf[0:share, 0:D] = unit.astype(BF16)
         buf[0:share, D : 2 * D] = tangent.astype(BF16)
         hi, lo = split_hi(ratio)
@@ -311,8 +323,8 @@
             gi[at, H:D] += got[:, 0 : D - H].astype(F32)
             gi[at, D:DX] += decoded(got[:, D - H : H])
 
-    def to_sibling():
-        for g in range(4):
+    def to_sibling(first, last):
+        for g in range(first, last):
             def one(q, carry):
                 sums_out(pl.multiple_of(half + (4 * g + q) * share, share))
                 return carry
@@ -350,12 +362,15 @@
     blocks(0, sigma, 2, 4)
     text_sums(0)
     sigma = prepare(1)
-    blocks(1, sigma, 2, 4)
-    to_sibling()
-    blocks(1, sigma, 0, 2)
+    blocks(1, sigma, 2, 3)
+    to_sibling(0, 2)
+    blocks(1, sigma, 3, 4)
+    to_sibling(2, 4)
 
     near = (0,) + AWAY
     for g in range(4):
+        if g % 2 == 0:
+            blocks(1, sigma, g // 2, g // 2 + 1)
         arrived(sib_got.at[pl.ds(4 * g * share, 4 * share), :], gr.at[g])
         for q in range(4 * g, 4 * g + 4):
             qa = pl.ds(q * share, share)
@@ -394,17 +409,16 @@
 
     for q in range(1, 8):
         arrived(rt_buf.at[q], rtr.at[q])
-    for q in range(6):
-        arrived(next_got.at[q], rir.at[24 + q])
-        add_in(0, q // 3, next_got[q])
-
     iu, it = img[0:share, 0:D].astype(F32), img[0:share, D : 2 * D].astype(F32)
     tu, tt = txt[0:share, 0:D].astype(F32), txt[0:share, D : 2 * D].astype(F32)
     pair_cos = jnp.sum(iu * tu, axis=1, keepdims=True)
     pair_cross = jnp.sum(it * tu + iu * tt, axis=1, keepdims=True)
     tmp[...] = jnp.zeros_like(tmp)
-    for k in range(2):
+    for k in (1, 0):
         if k == 0:
+            for q in range(6):
+                arrived(next_got.at[q], rir.at[24 + q])
+                add_in(0, q // 3, next_got[q])
             total = gi[0:share, 0:D]
             inner = gi[0:share, D : D + 1]
             inner_rate = gi[0:share, D + 1 : D + 2]
@@ -419,11 +433,11 @@
             ends = term[:, D:DX].astype(F32)
             inner = inner + (ends[:, 0:1] + ends[:, 2:3])
             inner_rate = inner_rate + (ends[:, 1:2] + ends[:, 3:4])
-        unit, tangent, radius, ratio = unit_parts(raw[2 * k], raw[2 * k + 1])
+        unit, tangent, inverse, ratio = unit_parts(raw[2 * k], raw[2 * k + 1])
         total = s * (total + (ratio * other - other_tangent))
         inner = s * (inner - pair_cos)
         inner_rate = s * (inner_rate - pair_cross)
-        back = (total - tangent * inner - unit * (inner_rate - ratio * inner)) / radius
+        back = (total - tangent * inner - unit * (inner_rate - ratio * inner)) * inverse
         hi, lo = split_hi(back)
         raw[2 * k] = hi.astype(F32)
         raw[2 * k + 1] = lo.astype(F32)
@@ -457,7 +471,7 @@
     per = 128 // T2
     places = [(W + 8 * (j // per), T2 * (j % per)) for j in range(W // 8)]
 
-    def pack(d, carry):
+    def pack(d):
         hp[d, 0:W, :] = hv[pl.ds(pl.multiple_of(d * W, 8), W), 0:128]
         packed = {}
         for j, (row, start) in enumerate(places):
@@ -467,12 +481,12 @@
             packed[row] = jnp.where((lane >= start) & (lane < start + T2), part, packed.get(row, jnp.zeros((8, 128), F32)))
         for row, value in packed.items():
             hp[d, row : row + 8, :] = value
-        return carry
-
-    lax.fori_loop(0, 16, pack, 0)
-    for q in range(1, 16):
+
+    for q in (8, 7, 9, 6, 10, 5, 11, 4, 12, 3, 13, 2, 14, 1, 15):
         to = (dp + q) % 16
+        pack(to)
         send(hp.at[to], hv_got.at[16 - q], hs.at[q], hr.at[16 - q], (to, tp))
+    pack(dp)
     total = hp[dp]
     for q in range(1, 16):
         arrived(hv_got.at[q], hr.at[q])
@@ -502,9 +516,12 @@
         return pl.pallas_call(
             functools.partial(kernel, nz, nx, D, W),
             out_shape=[jax.ShapeDtypeStruct((W, W), F32)] * 2,
-            in_specs=[vmem] * 6 + [pl.BlockSpec(memory_space=pltpu.SMEM)] * 2,
+            in_specs=[pl.BlockSpec(memory_space=pl.ANY)] * 2 + [vmem] * 4 + [pl.BlockSpec(memory_space=pltpu.SMEM)] * 2,
             out_specs=[vmem] * 2,
             scratch_shapes=[
+                pltpu.VMEM((rows, D), BF16),
+                pltpu.VMEM((rows, D), BF16),
+                sem(2),
                 pltpu.VMEM((640, D), BF16),
                 pltpu.VMEM((rows, 384), BF16),
                 pltpu.VMEM((16, share, 384), BF16),

time: 132 us -> 128 us (0.970)
  Pallas kernels: 127 us -> 123 us
    pallas_call x1, Pallas kernels: 127 us -> 123 us  [local(): pl.pallas_call(functools.partial(kernel, nz, nx, D, W), out_shape=[jax.Sh...]
where the time goes in v5:
time: 128 us
  Pallas kernels  123 us (96%)
  local copies, waits for them, and re-layouts  2.77 us (2%)
  between operations  1.93 us (2%)
    pallas_call x1, Pallas kernels, local(): pl.pallas_call(functools.partial(kernel, nz, nx, D, W), out_shape=[jax.Sh...  123 us
    unnamed x2, local copies, waits for them, and re-layouts  2.77 us

profile of v5, /device:TPU:1, one launch (start us, length us, event | category | flops | bytes accessed | tf_op | source)
XLA Modules:
  0.0 127.8 jit_solution(15304704476053131712)
XLA Ops:
  1.9 123.1 %shard_map.95 = (f32[72,72]{1,0:T(8,128)}, f32[72,72]{1,0:T(8,128)}) custom-call(bf16[768,1152]{1,0:T(8,128)(2,1)} %from_i.1, bf16[768,1152]{1,0:T(8,128)(2,1)} %from_t.1, bf16[72,1152]{1,0:T(8,128)(2,1)} %bitcast.4, bf16[72,1152]{1,0:T(8,128)(2,1)} %bitcast.5, bf16[72,1152]{1,0:T(8,128)(2,1)} %bitcast.6, bf16[72,1152]{1,0:T(8,128)(2,1)} %bitcast.7, ...), custom_call_target="tpu_custom_call" | custom-call | tf_op jit(solution)/shard_map/pallas_call | solution.py:516
  125.1 1.4 %copy.14 = f32[72,72]{1,0:T(8,128)} copy(f32[72,72]{1,0:T(8,128)} %get-tuple-element.4) | data formatting | bytes 41472
  126.5 1.4 %copy.15 = f32[72,72]{1,0:T(8,128)} copy(f32[72,72]{1,0:T(8,128)} %get-tuple-element.5) | data formatting | bytes 41472

commit v6 on v5

--- a/solution.py
+++ b/solution.py
@@ -251,10 +251,10 @@
     RB = 8 * share
 
     def prepare(ci):
-        csum[...] = jnp.zeros_like(csum)
+        csum[ci] = jnp.zeros((8, TC), F32)
         return dot_nt(first_two, txt[ci * TC : (ci + 1) * TC, 2 * D : DE])[0:1, :]
 
-    def blocks(ci, sigma, low, high):
+    def blocks(ci, sigma, low, high, first):
         at = pl.ds(ci * TC, TC)
 
         def block(r, carry):
@@ -272,13 +272,13 @@
             pb = prob.astype(BF16)
             q1 = prob * cosine
             q2 = prob * cross + rate * cosine
-            csum[0:1, :] += jnp.sum(q1, axis=0, keepdims=True)
-            csum[1:2, :] += jnp.sum(q2, axis=0, keepdims=True)
-            pb_buf[ra, :] = pb
-            at_buf[ra, :] = (rate - sigma * prob).astype(BF16)
+            csum[ci, 0:1, :] += jnp.sum(q1, axis=0, keepdims=True)
+            csum[ci, 1:2, :] += jnp.sum(q2, axis=0, keepdims=True)
+            pb_buf[ci, ra, :] = pb
+            at_buf[ci, ra, :] = (rate - sigma * prob).astype(BF16)
             gain = dot_nn((rate - rho * prob).astype(BF16), tu) + dot_nn(pb, tt)
             sums = lanes_of((jnp.sum(q1, axis=1, keepdims=True), jnp.sum(q2, axis=1, keepdims=True)), RB)
-            if ci == 0:
+            if first:
                 gi[ra, 0:D] = gain
                 gi[ra, D:DX] = sums
             else:
@@ -290,12 +290,12 @@
 
     def text_sums(ci):
         at = pl.ds(ci * TC, TC)
-        hi, lo = split_hi(csum[...])
+        hi, lo = split_hi(csum[ci])
         tops = jnp.concatenate([hi[0:2].astype(F32), lo[0:2].astype(F32), jnp.zeros((4, TC), F32)], axis=0)
         st_buf[at, D:DX] = dot_tn(tops.astype(BF16), eye).astype(BF16)
         for k in range(0, D, 256):
             e = min(k + 256, D)
-            gain = dot_tn(at_buf[...], img[:, k:e]) + dot_tn(pb_buf[...], img[:, D + k : D + e])
+            gain = dot_tn(at_buf[ci], img[:, k:e]) + dot_tn(pb_buf[ci], img[:, D + k : D + e])
             st_buf[at, k:e] = gain.astype(BF16)
         for q in range(4 * ci, 4 * ci + 4):
             if q > 0:
@@ -342,6 +342,8 @@
     for back in (2, -2):
         twait(back)
         t_on(back)
+    near_sigma = prepare(1)
+    blocks(1, near_sigma, 0, 1, True)
     for pos in XY_SLOTS[8:11]:
         i_step(pos)
     for back in (3, -3):
@@ -352,25 +354,24 @@
         i_step(pos)
     twait(4)
     sigma = prepare(0)
-    blocks(0, sigma, 0, 1)
+    blocks(0, sigma, 0, 1, False)
     for pos in XY_SLOTS[15:16]:
         i_step(pos)
-    blocks(0, sigma, 1, 2)
+    blocks(1, near_sigma, 1, 2, True)
+    blocks(0, sigma, 1, 2, False)
     for slot in range(16):
         for part in (0, 1):
             arrived(ipart(16 + slot, part), air.at[part * 32 + 16 + slot])
-    blocks(0, sigma, 2, 4)
+    blocks(0, sigma, 2, 4, True)
     text_sums(0)
-    sigma = prepare(1)
-    blocks(1, sigma, 2, 3)
+    blocks(1, near_sigma, 2, 3, False)
     to_sibling(0, 2)
-    blocks(1, sigma, 3, 4)
+    blocks(1, near_sigma, 3, 4, False)
     to_sibling(2, 4)
+    text_sums(1)
 
     near = (0,) + AWAY
     for g in range(4):
-        if g % 2 == 0:
-            blocks(1, sigma, g // 2, g // 2 + 1)
         arrived(sib_got.at[pl.ds(4 * g * share, 4 * share), :], gr.at[g])
         for q in range(4 * g, 4 * g + 4):
             qa = pl.ds(q * share, share)
@@ -385,7 +386,6 @@
                     at = part * 12 + AWAY.index(mirrored(off, 4)) * 4 + near.index(keep)
                     to = device_at(0, dy, 0, c) if part == 0 else device_at(0, 0, dx, c)
                     rsend(si_buf.at[qa, halves[part]], first_got.at[at], at, to)
-    text_sums(1)
     for keep in AWAY + (0,):
         for part in (0, 1):
             row = XY_SLOTS.index((keep, 0) if part == 0 else (0, keep)) * share
@@ -529,9 +529,9 @@
                 pltpu.VMEM((32 * share, DE), BF16),
                 pltpu.VMEM((8 * share, DE), BF16),
                 pltpu.VMEM((32 * share, DX), F32),
-                pltpu.VMEM((32 * share, 4 * share), BF16),
-                pltpu.VMEM((32 * share, 4 * share), BF16),
-                pltpu.VMEM((8, 4 * share), F32),
+                pltpu.VMEM((2, 32 * share, 4 * share), BF16),
+                pltpu.VMEM((2, 32 * share, 4 * share), BF16),
+                pltpu.VMEM((2, 8, 4 * share), F32),
                 pltpu.VMEM((32 * share, DX), BF16),
                 pltpu.VMEM((8 * share, DX), BF16),
                 pltpu.VMEM((16 * share, DX), BF16),

time: 128 us -> 128 us (level)
  no operation moved by 1% of the time
where the time goes in v6:
time: 128 us
  Pallas kernels  123 us (96%)
  local copies, waits for them, and re-layouts  2.77 us (2%)
  between operations  1.93 us (2%)
    pallas_call x1, Pallas kernels, local(): pl.pallas_call(functools.partial(kernel, nz, nx, D, W), out_shape=[jax.Sh...  123 us
    unnamed x2, local copies, waits for them, and re-layouts  2.77 us

profile of v6, /device:TPU:1, one launch (start us, length us, event | category | flops | bytes accessed | tf_op | source)
XLA Modules:
  0.0 127.7 jit_solution(7953149304148088890)
XLA Ops:
  1.9 123.0 %shard_map.95 = (f32[72,72]{1,0:T(8,128)}, f32[72,72]{1,0:T(8,128)}) custom-call(bf16[768,1152]{1,0:T(8,128)(2,1)} %from_i.1, bf16[768,1152]{1,0:T(8,128)(2,1)} %from_t.1, bf16[72,1152]{1,0:T(8,128)(2,1)} %bitcast.4, bf16[72,1152]{1,0:T(8,128)(2,1)} %bitcast.5, bf16[72,1152]{1,0:T(8,128)(2,1)} %bitcast.6, bf16[72,1152]{1,0:T(8,128)(2,1)} %bitcast.7, ...), custom_call_target="tpu_custom_call" | custom-call | tf_op jit(solution)/shard_map/pallas_call | solution.py:516
  124.9 1.4 %copy.14 = f32[72,72]{1,0:T(8,128)} copy(f32[72,72]{1,0:T(8,128)} %get-tuple-element.4) | data formatting | bytes 41472
  126.3 1.4 %copy.15 = f32[72,72]{1,0:T(8,128)} copy(f32[72,72]{1,0:T(8,128)} %get-tuple-element.5) | data formatting | bytes 41472

commit v7 on v6

--- a/solution.py
+++ b/solution.py
@@ -448,8 +448,11 @@
             tmp[:, 256 + 32 * k : 256 + 32 * k + T2] = raw[2 + k, :, q * W + T1 : (q + 1) * W]
         stage[q] = tmp[...].astype(BF16)
 
-    for q in range(1, 16):
-        send(stage.at[tp_ids[q]], cols.at[share_at(tp), :], bs.at[q], br.at[tp], (dp, tp_ids[q]))
+    for step in range(2):
+        side = 1 - tp // 8 if step == 0 else tp // 8
+        for q in range(step, 8):
+            to = side * 8 + (tp + q) % 8
+            send(stage.at[to], cols.at[share_at(tp), :], bs.at[step * 8 + q], br.at[tp], (dp, to))
     cols[share_at(tp), :] = stage[pl.ds(tp, 1)].reshape(share, 384)
     for q in range(1, 16):
         arrived(cols.at[share_at(tp_ids[q]), :], br.at[tp_ids[q]])

time: 128 us -> 128 us (level)
  no operation moved by 1% of the time
where the time goes in v7:
time: 128 us
  Pallas kernels  123 us (96%)
  local copies, waits for them, and re-layouts  2.77 us (2%)
  between operations  1.93 us (2%)
    pallas_call x1, Pallas kernels, local(): pl.pallas_call(functools.partial(kernel, nz, nx, D, W), out_shape=[jax.Sh...  123 us
    unnamed x2, local copies, waits for them, and re-layouts  2.77 us

profile of v7, /device:TPU:1, one launch (start us, length us, event | category | flops | bytes accessed | tf_op | source)
XLA Modules:
  0.0 127.7 jit_solution(14931943220658848002)
XLA Ops:
  1.9 123.0 %shard_map.95 = (f32[72,72]{1,0:T(8,128)}, f32[72,72]{1,0:T(8,128)}) custom-call(bf16[768,1152]{1,0:T(8,128)(2,1)} %from_i.1, bf16[768,1152]{1,0:T(8,128)(2,1)} %from_t.1, bf16[72,1152]{1,0:T(8,128)(2,1)} %bitcast.4, bf16[72,1152]{1,0:T(8,128)(2,1)} %bitcast.5, bf16[72,1152]{1,0:T(8,128)(2,1)} %bitcast.6, bf16[72,1152]{1,0:T(8,128)(2,1)} %bitcast.7, ...), custom_call_target="tpu_custom_call" | custom-call | tf_op jit(solution)/shard_map/pallas_call | solution.py:519
  125.0 1.4 %copy.14 = f32[72,72]{1,0:T(8,128)} copy(f32[72,72]{1,0:T(8,128)} %get-tuple-element.4) | data formatting | bytes 41472
  126.4 1.4 %copy.15 = f32[72,72]{1,0:T(8,128)} copy(f32[72,72]{1,0:T(8,128)} %get-tuple-element.5) | data formatting | bytes 41472
